TPU v7x, 256 devices: a whole 4x4x8 slice. The times are simulated.
256 devices in a mesh: blk: 32 (over x, z_lo, core), head: 8 (over y, z_hi).
Axes of the slice: x: 4, y: 4, z: 8 (z_hi: 2, z_lo: 4; z = z_hi * 4 + z_lo), core: 2. Of those that a mesh axis runs over, the one named last changes fastest.
Arguments:
- query: bfloat16 [8, 16384, 128], P('head', 'blk'), may hold values from -12 to 12
- key: bfloat16 [16384, 128], P('blk'), may hold values from -6 to 6
- value: bfloat16 [16384, 128], P('blk'), may hold values from -6 to 6
- output: bfloat16 [8, 16384, 128], P('head', 'blk'), may hold values from -6 to 6
- out_grad: bfloat16 [8, 16384, 128], P('head', 'blk'), may hold values from -6 to 6
- lse: float32 [8, 16384], P('head', 'blk'), may hold values from 5 to 14
- block_order: int32 [64], replicated, may hold values from 0 to 63, as said below
Outputs:
- grad_query: float32 [8, 16384, 128], P('head', 'blk')
- grad_key: float32 [16384, 128], P(('blk', 'head'))
- grad_value: float32 [16384, 128], P(('blk', 'head'))
Inputs may be any that keep to these rules, and one draw needn't show every extreme that they name: A permutation of 0 to 63; the storage block j, rows j * 256 to (j + 1) * 256 - 1, holds the sequence block block_order[j].
All inputs are finite; a program needn't handle non-finite values.
Results may differ from a plain program's by a relative error of at most 0.0036.
Values may be sent and summed in bfloat16 or wider, within the bound.
A program may use at most 64 MiB of HBM per device.

v0:
```python
import jax
import jax.numpy as jnp
from jax import lax
from jax.sharding import PartitionSpec as P


def passed_along(block, axis, distance):
    devices = range(lax.axis_size(axis))
    route = [((i - distance) % len(devices), i) for i in devices]
    return lax.ppermute(block, axis, route)


def in_blocks(shard, dim, length):
    dims = shard.shape
    pieces = shard.reshape(*dims[:dim], length, dims[dim] // length, *dims[dim + 1 :])
    return jnp.moveaxis(pieces, dim, 0)


def sum_at_owner(shard, axis, dim):
    pieces = in_blocks(shard, dim, lax.axis_size(axis))
    arrived = lax.all_to_all(pieces, axis, split_axis=0, concat_axis=0, tiled=True)
    return arrived.sum(axis=0)


def side_by_side(arrays, axis, dim, along):
    ends, at = ([], 0)
    for a in arrays[:-1]:
        at += a.shape[along]
        ends.append(at)
    both = jnp.concatenate(arrays, axis=along)
    return tuple(jnp.split(sum_at_owner(both, axis, dim), ends, axis=along))


def inner(left, right):
    return lax.dot_general(
        left, right, (((1,), (1,)), ((), ())), preferred_element_type=jnp.float32
    )


def outer(left, right):
    return lax.dot_general(
        left, right, (((0,), (0,)), ((), ())), preferred_element_type=jnp.float32
    )


def tile_grads(q_rows, g_rows, l_rows, d_rows, q_pos, key, value, k_pos, scale):
    scores = inner(q_rows, key) * scale
    live = q_pos[:, None] >= k_pos[None, :]
    probs = jnp.where(live, jnp.exp(scores - l_rows[:, None]), 0.0)
    probs_low = probs.astype(jnp.bfloat16)
    dprobs = inner(g_rows, value)
    dscores = (probs * (dprobs - d_rows[:, None])).astype(jnp.bfloat16)
    grad_q = jnp.dot(dscores, key, preferred_element_type=jnp.float32) * scale
    grad_k = outer(dscores, q_rows) * scale
    grad_v = outer(probs_low, g_rows)
    return (grad_q, grad_k, grad_v)


def on_device(query, key, value, output, out_grad, lse, block_order):
    scale = key.shape[1] ** (-0.5)
    rows = key.shape[0]
    half = rows // 2
    devices = lax.axis_size("blk")
    mine = lax.axis_index("blk")
    q_rows = query[0]
    g_rows = out_grad[0]
    l_rows = lse[0]
    d_rows = jnp.sum(g_rows.astype(jnp.float32) * output[0].astype(jnp.float32), axis=1)
    offsets = jnp.arange(half, dtype=jnp.int32)

    def place(block):
        return lax.dynamic_index_in_dim(block_order, block, 0, keepdims=False) * half + offsets

    k_pos = jnp.concatenate([place(2 * mine), place(2 * mine + 1)])
    zeros = jnp.zeros(key.shape, jnp.float32)

    def visit(q_vis, g_vis, l_vis, d_vis, q_pos, grad_k, grad_v):
        part_q, part_k, part_v = tile_grads(
            q_vis, g_vis, l_vis, d_vis, q_pos, key, value, k_pos, scale
        )
        return (part_q, grad_k + part_k, grad_v + part_v)

    def turn(step, carry):
        q_vis, g_vis, dq_vis, l_vis, d_vis, grad_k, grad_v = carry
        source = (mine - step) % devices
        q_pos = jnp.concatenate([place(2 * source), place(2 * source + 1)])
        part_q, grad_k, grad_v = visit(q_vis, g_vis, l_vis, d_vis, q_pos, grad_k, grad_v)
        q_vis, g_vis = passed_along((q_vis, g_vis), "blk", 1)
        dq_vis, l_vis, d_vis = passed_along((dq_vis + part_q, l_vis, d_vis), "blk", 1)
        return (q_vis, g_vis, dq_vis, l_vis, d_vis, grad_k, grad_v)

    start = (q_rows, g_rows, zeros, l_rows, d_rows, zeros, zeros)
    final = lax.fori_loop(0, devices, turn, start)
    grad_q = final[2]
    grad_k = final[5]
    grad_v = final[6]
    own_k, own_v = side_by_side((grad_k, grad_v), "head", 0, 1)
    return (grad_q[None], own_k, own_v)


def solution(mesh):
    in_specs = (
        P("head", "blk", None),
        P("blk", None),
        P("blk", None),
        P("head", "blk", None),
        P("head", "blk", None),
        P("head", "blk"),
        P(),
    )
    out_specs = (P("head", "blk", None), P(("blk", "head"), None), P(("blk", "head"), None))
    return jax.shard_map(
        on_device, mesh=mesh, in_specs=in_specs, out_specs=out_specs, check_vma=False
    )
```

profile of v0, /device:TPU:39, one launch (start us, length us, event | category | flops | bytes accessed | tf_op | source)
XLA Modules:
  0.0 463.8 jit_solution(1278539646444129148)
XLA Ops:
  5.2 428.5 %while.29 = (s32[]{:T(128)}, bf16[512,128]{1,0:T(8,128)(2,1)S(1)}, bf16[512,128]{1,0:T(8,128)(2,1)S(1)}, f32[512,128]{1,0:T(8,128)S(1)}, f32[512]{0:T(512)S(1)},...) while((s32[]{:T(128)}, bf16[512,128]{1,0:T(8,128)(2,1)S(1)}, ...), condition=%wide.region_2.3_spmd.clone.clone, body=%wide.region_1.2_spmd.clone.clone.sunk | while | flops 338101280 | bytes 9869981 | solution.py:93
  14.3 2.5 collective-permute-done.2
  22.7 6.0 %collective-permute-start.2 = (f32[512,128]{1,0:T(8,128)S(1)}, f32[512,128]{1,0:T(8,128)S(1)}, u32[]{:S(2)}, u32[]{:S(2)}) collective-permute-start(f32[512,128]{1,0:T(8,128)S(1)} %fusion.51), channel_id=1, source_target_pairs={{248,0},{0,8},{8,16},{16,24},{24,32},{32,40},{40,48},{48,56},{56,6... | collective-permute-start | bytes 786440 | tf_op jit(solution)/shard_map/while/body/eval_jaxpr/ppermute | solution.py:10
  29.5 2.5 collective-permute-done.2
  37.7 4.0 collective-permute-start.2
  50.6 4.9 %collective-permute-start.2 = (f32[512,128]{1,0:T(8,128)S(1)}, f32[512,128]{1,0:T(8,128)S(1)}, u32[]{:S(2)}, u32[]{:S(2)}) collective-permute-start(f32[512,128]{1,0:T(8,128)S(1)} %fusion.51), channel_id=1, source_target_pairs={{248,0},{0,8},{8,16},{16,24},{24,32},{32,40},{40,48},{48,56},{56,6... | collective-permute-start | bytes 786440 | tf_op jit(solution)/shard_map/while/body/eval_jaxpr/ppermute | solution.py:10
  56.3 2.5 collective-permute-done.2
  64.5 3.9 collective-permute-start.2
  77.4 4.8 %collective-permute-start.2 = (f32[512,128]{1,0:T(8,128)S(1)}, f32[512,128]{1,0:T(8,128)S(1)}, u32[]{:S(2)}, u32[]{:S(2)}) collective-permute-start(f32[512,128]{1,0:T(8,128)S(1)} %fusion.51), channel_id=1, source_target_pairs={{248,0},{0,8},{8,16},{16,24},{24,32},{32,40},{40,48},{48,56},{56,6... | collective-permute-start | bytes 786440 | tf_op jit(solution)/shard_map/while/body/eval_jaxpr/ppermute | solution.py:10
  83.1 2.5 collective-permute-done.2
  91.3 3.9 collective-permute-start.2
  96.1 2.5 collective-permute-done.2
  104.3 4.6 collective-permute-start.2
  109.7 2.5 collective-permute-done.2
  117.8 3.9 collective-permute-start.2
  122.6 2.5 collective-permute-done.2
  130.8 5.0 %collective-permute-start.2 = (f32[512,128]{1,0:T(8,128)S(1)}, f32[512,128]{1,0:T(8,128)S(1)}, u32[]{:S(2)}, u32[]{:S(2)}) collective-permute-start(f32[512,128]{1,0:T(8,128)S(1)} %fusion.51), channel_id=1, source_target_pairs={{248,0},{0,8},{8,16},{16,24},{24,32},{32,40},{40,48},{48,56},{56,6... | collective-permute-start | bytes 786440 | tf_op jit(solution)/shard_map/while/body/eval_jaxpr/ppermute | solution.py:10
  136.7 2.5 collective-permute-done.2
  144.9 3.9 collective-permute-start.2
  149.6 2.5 collective-permute-done.2
  157.8 4.8 %collective-permute-start.2 = (f32[512,128]{1,0:T(8,128)S(1)}, f32[512,128]{1,0:T(8,128)S(1)}, u32[]{:S(2)}, u32[]{:S(2)}) collective-permute-start(f32[512,128]{1,0:T(8,128)S(1)} %fusion.51), channel_id=1, source_target_pairs={{248,0},{0,8},{8,16},{16,24},{24,32},{32,40},{40,48},{48,56},{56,6... | collective-permute-start | bytes 786440 | tf_op jit(solution)/shard_map/while/body/eval_jaxpr/ppermute | solution.py:10
  163.5 2.5 collective-permute-done.2
  171.7 3.9 collective-permute-start.2
  176.5 2.5 collective-permute-done.2
  184.6 4.8 %collective-permute-start.2 = (f32[512,128]{1,0:T(8,128)S(1)}, f32[512,128]{1,0:T(8,128)S(1)}, u32[]{:S(2)}, u32[]{:S(2)}) collective-permute-start(f32[512,128]{1,0:T(8,128)S(1)} %fusion.51), channel_id=1, source_target_pairs={{248,0},{0,8},{8,16},{16,24},{24,32},{32,40},{40,48},{48,56},{56,6... | collective-permute-start | bytes 786440 | tf_op jit(solution)/shard_map/while/body/eval_jaxpr/ppermute | solution.py:10
  190.3 2.5 collective-permute-done.2
  198.5 3.9 collective-permute-start.2
  203.3 2.5 collective-permute-done.2
  211.5 4.6 collective-permute-start.2
  216.8 2.5 collective-permute-done.2
  225.0 3.9 collective-permute-start.2
  229.8 2.5 collective-permute-done.2
  238.0 5.0 %collective-permute-start.2 = (f32[512,128]{1,0:T(8,128)S(1)}, f32[512,128]{1,0:T(8,128)S(1)}, u32[]{:S(2)}, u32[]{:S(2)}) collective-permute-start(f32[512,128]{1,0:T(8,128)S(1)} %fusion.51), channel_id=1, source_target_pairs={{248,0},{0,8},{8,16},{16,24},{24,32},{32,40},{40,48},{48,56},{56,6... | collective-permute-start | bytes 786440 | tf_op jit(solution)/shard_map/while/body/eval_jaxpr/ppermute | solution.py:10
  243.9 2.5 collective-permute-done.2
  252.0 3.9 collective-permute-start.2
  256.8 2.5 collective-permute-done.2
  265.0 4.8 %collective-permute-start.2 = (f32[512,128]{1,0:T(8,128)S(1)}, f32[512,128]{1,0:T(8,128)S(1)}, u32[]{:S(2)}, u32[]{:S(2)}) collective-permute-start(f32[512,128]{1,0:T(8,128)S(1)} %fusion.51), channel_id=1, source_target_pairs={{248,0},{0,8},{8,16},{16,24},{24,32},{32,40},{40,48},{48,56},{56,6... | collective-permute-start | bytes 786440 | tf_op jit(solution)/shard_map/while/body/eval_jaxpr/ppermute | solution.py:10
  270.7 2.5 collective-permute-done.2
  278.9 3.9 collective-permute-start.2
  283.6 2.5 collective-permute-done.2
  291.8 4.8 %collective-permute-start.2 = (f32[512,128]{1,0:T(8,128)S(1)}, f32[512,128]{1,0:T(8,128)S(1)}, u32[]{:S(2)}, u32[]{:S(2)}) collective-permute-start(f32[512,128]{1,0:T(8,128)S(1)} %fusion.51), channel_id=1, source_target_pairs={{248,0},{0,8},{8,16},{16,24},{24,32},{32,40},{40,48},{48,56},{56,6... | collective-permute-start | bytes 786440 | tf_op jit(solution)/shard_map/while/body/eval_jaxpr/ppermute | solution.py:10
  297.5 2.5 collective-permute-done.2
  305.7 3.9 collective-permute-start.2
  310.5 2.5 collective-permute-done.2
  318.7 4.6 collective-permute-start.2
  324.0 2.5 collective-permute-done.2
  332.2 3.9 collective-permute-start.2
  337.0 2.5 collective-permute-done.2
  345.2 5.0 %collective-permute-start.2 = (f32[512,128]{1,0:T(8,128)S(1)}, f32[512,128]{1,0:T(8,128)S(1)}, u32[]{:S(2)}, u32[]{:S(2)}) collective-permute-start(f32[512,128]{1,0:T(8,128)S(1)} %fusion.51), channel_id=1, source_target_pairs={{248,0},{0,8},{8,16},{16,24},{24,32},{32,40},{40,48},{48,56},{56,6... | collective-permute-start | bytes 786440 | tf_op jit(solution)/shard_map/while/body/eval_jaxpr/ppermute | solution.py:10
  351.1 2.5 collective-permute-done.2
  359.2 3.9 collective-permute-start.2
  364.0 2.5 collective-permute-done.2
  372.2 4.8 %collective-permute-start.2 = (f32[512,128]{1,0:T(8,128)S(1)}, f32[512,128]{1,0:T(8,128)S(1)}, u32[]{:S(2)}, u32[]{:S(2)}) collective-permute-start(f32[512,128]{1,0:T(8,128)S(1)} %fusion.51), channel_id=1, source_target_pairs={{248,0},{0,8},{8,16},{16,24},{24,32},{32,40},{40,48},{48,56},{56,6... | collective-permute-start | bytes 786440 | tf_op jit(solution)/shard_map/while/body/eval_jaxpr/ppermute | solution.py:10
  377.9 2.5 collective-permute-done.2
  386.1 3.9 collective-permute-start.2
  390.8 2.5 collective-permute-done.2
  399.0 4.8 %collective-permute-start.2 = (f32[512,128]{1,0:T(8,128)S(1)}, f32[512,128]{1,0:T(8,128)S(1)}, u32[]{:S(2)}, u32[]{:S(2)}) collective-permute-start(f32[512,128]{1,0:T(8,128)S(1)} %fusion.51), channel_id=1, source_target_pairs={{248,0},{0,8},{8,16},{16,24},{24,32},{32,40},{40,48},{48,56},{56,6... | collective-permute-start | bytes 786440 | tf_op jit(solution)/shard_map/while/body/eval_jaxpr/ppermute | solution.py:10
  404.7 2.5 collective-permute-done.2
  412.9 3.9 collective-permute-start.2
  417.7 2.5 collective-permute-done.2
  425.8 4.6 collective-permute-start.2
  431.2 2.5 collective-permute-done.2
  434.5 9.0 %all-to-all-start = ((f32[8,64,256]{2,1,0:T(8,128)}), f32[8,64,256]{2,1,0:T(8,128)S(1)}, u32[]{:S(2)}, u32[]{:S(2)}) async-start(f32[8,64,256]{2,1,0:T(8,128)} %bitcast.7), calls=%async_computation | async-start | bytes 1048576 | tf_op jit(solution)/shard_map/all_to_all | solution.py:21
  443.5 18.9 %all-to-all-done = f32[8,64,256]{2,1,0:T(8,128)S(1)} async-done(((f32[8,64,256]{2,1,0:T(8,128)}), f32[8,64,256]{2,1,0:T(8,128)S(1)}, u32[]{:S(2)}, u32[]{:S(2)}) %all-to-all-start) | async-done | bytes 524320 | tf_op jit(solution)/shard_map/all_to_all | solution.py:21
  (667 shorter events, 180.2 us)
Async XLA Ops:
  5.2 9.1 %collective-permute-start.3 = (f32[512]{0:T(512)S(1)}, f32[512]{0:T(512)S(1)}, u32[]{:S(2)}, u32[]{:S(2)}) collective-permute-start(f32[512]{0:T(512)S(1)} %copy.22), channel_id=1, source_target_pairs={{248,0},{0,8},{8,16},{16,24},{24,32},{32,40},{40,48},{48,56},{56,6... | collective-permute-start | bytes 6152 | tf_op jit(solution)/shard_map/while/body/eval_jaxpr/ppermute | solution.py:10
  16.8 12.6 %collective-permute-start.3 = (f32[512]{0:T(512)S(1)}, f32[512]{0:T(512)S(1)}, u32[]{:S(2)}, u32[]{:S(2)}) collective-permute-start(f32[512]{0:T(512)S(1)} %copy.22), channel_id=1, source_target_pairs={{248,0},{0,8},{8,16},{16,24},{24,32},{32,40},{40,48},{48,56},{56,6... | collective-permute-start | bytes 6152 | tf_op jit(solution)/shard_map/while/body/eval_jaxpr/ppermute | solution.py:10
  19.3 10.2 %collective-permute-start.4 = (f32[512]{0:T(512)S(1)}, f32[512]{0:T(512)S(1)}, u32[]{:S(2)}, u32[]{:S(2)}) collective-permute-start(f32[512]{0:T(512)S(1)} %copy.23), channel_id=1, source_target_pairs={{248,0},{0,8},{8,16},{16,24},{24,32},{32,40},{40,48},{48,56},{56,6... | collective-permute-start | bytes 6152 | tf_op jit(solution)/shard_map/while/body/eval_jaxpr/ppermute | solution.py:10
  19.4 10.1 %collective-permute-start = (bf16[512,128]{1,0:T(8,128)(2,1)S(1)}, bf16[512,128]{1,0:T(8,128)(2,1)S(1)}, u32[]{:S(2)}, u32[]{:S(2)}) collective-permute-start(bf16[512,128]{1,0:T(8,128)(2,1)S(1)} %copy.19), channel_id=1, source_target_pairs={{248,0},{0,8},{8,16},{16,24},{24,32},{32,40},{40,48},{48,56},{56,6... | collective-permute-start | bytes 393224 | tf_op jit(solution)/shard_map/while/body/eval_jaxpr/ppermute | solution.py:10
  19.7 9.8 %collective-permute-start.1 = (bf16[512,128]{1,0:T(8,128)(2,1)S(1)}, bf16[512,128]{1,0:T(8,128)(2,1)S(1)}, u32[]{:S(2)}, u32[]{:S(2)}) collective-permute-start(bf16[512,128]{1,0:T(8,128)(2,1)S(1)} %copy.20), channel_id=1, source_target_pairs={{248,0},{0,8},{8,16},{16,24},{24,32},{32,40},{40,48},{48,56},{56,6... | collective-permute-start | bytes 393224 | tf_op jit(solution)/shard_map/while/body/eval_jaxpr/ppermute | solution.py:10
  22.7 9.3 %collective-permute-start.2 = (f32[512,128]{1,0:T(8,128)S(1)}, f32[512,128]{1,0:T(8,128)S(1)}, u32[]{:S(2)}, u32[]{:S(2)}) collective-permute-start(f32[512,128]{1,0:T(8,128)S(1)} %fusion.51), channel_id=1, source_target_pairs={{248,0},{0,8},{8,16},{16,24},{24,32},{32,40},{40,48},{48,56},{56,6... | collective-permute-start | bytes 786440 | tf_op jit(solution)/shard_map/while/body/eval_jaxpr/ppermute | solution.py:10
  32.0 10.4 %collective-permute-start.3 = (f32[512]{0:T(512)S(1)}, f32[512]{0:T(512)S(1)}, u32[]{:S(2)}, u32[]{:S(2)}) collective-permute-start(f32[512]{0:T(512)S(1)} %copy.22), channel_id=1, source_target_pairs={{248,0},{0,8},{8,16},{16,24},{24,32},{32,40},{40,48},{48,56},{56,6... | collective-permute-start | bytes 6152 | tf_op jit(solution)/shard_map/while/body/eval_jaxpr/ppermute | solution.py:10
  44.9 11.3 %collective-permute-start.3 = (f32[512]{0:T(512)S(1)}, f32[512]{0:T(512)S(1)}, u32[]{:S(2)}, u32[]{:S(2)}) collective-permute-start(f32[512]{0:T(512)S(1)} %copy.22), channel_id=1, source_target_pairs={{248,0},{0,8},{8,16},{16,24},{24,32},{32,40},{40,48},{48,56},{56,6... | collective-permute-start | bytes 6152 | tf_op jit(solution)/shard_map/while/body/eval_jaxpr/ppermute | solution.py:10
  47.4 8.9 %collective-permute-start.4 = (f32[512]{0:T(512)S(1)}, f32[512]{0:T(512)S(1)}, u32[]{:S(2)}, u32[]{:S(2)}) collective-permute-start(f32[512]{0:T(512)S(1)} %copy.23), channel_id=1, source_target_pairs={{248,0},{0,8},{8,16},{16,24},{24,32},{32,40},{40,48},{48,56},{56,6... | collective-permute-start | bytes 6152 | tf_op jit(solution)/shard_map/while/body/eval_jaxpr/ppermute | solution.py:10
  47.5 8.8 %collective-permute-start = (bf16[512,128]{1,0:T(8,128)(2,1)S(1)}, bf16[512,128]{1,0:T(8,128)(2,1)S(1)}, u32[]{:S(2)}, u32[]{:S(2)}) collective-permute-start(bf16[512,128]{1,0:T(8,128)(2,1)S(1)} %copy.19), channel_id=1, source_target_pairs={{248,0},{0,8},{8,16},{16,24},{24,32},{32,40},{40,48},{48,56},{56,6... | collective-permute-start | bytes 393224 | tf_op jit(solution)/shard_map/while/body/eval_jaxpr/ppermute | solution.py:10
  47.6 8.7 %collective-permute-start.1 = (bf16[512,128]{1,0:T(8,128)(2,1)S(1)}, bf16[512,128]{1,0:T(8,128)(2,1)S(1)}, u32[]{:S(2)}, u32[]{:S(2)}) collective-permute-start(bf16[512,128]{1,0:T(8,128)(2,1)S(1)} %copy.20), channel_id=1, source_target_pairs={{248,0},{0,8},{8,16},{16,24},{24,32},{32,40},{40,48},{48,56},{56,6... | collective-permute-start | bytes 393224 | tf_op jit(solution)/shard_map/while/body/eval_jaxpr/ppermute | solution.py:10
  58.8 10.4 %collective-permute-start.3 = (f32[512]{0:T(512)S(1)}, f32[512]{0:T(512)S(1)}, u32[]{:S(2)}, u32[]{:S(2)}) collective-permute-start(f32[512]{0:T(512)S(1)} %copy.22), channel_id=1, source_target_pairs={{248,0},{0,8},{8,16},{16,24},{24,32},{32,40},{40,48},{48,56},{56,6... | collective-permute-start | bytes 6152 | tf_op jit(solution)/shard_map/while/body/eval_jaxpr/ppermute | solution.py:10
  71.8 11.3 %collective-permute-start.3 = (f32[512]{0:T(512)S(1)}, f32[512]{0:T(512)S(1)}, u32[]{:S(2)}, u32[]{:S(2)}) collective-permute-start(f32[512]{0:T(512)S(1)} %copy.22), channel_id=1, source_target_pairs={{248,0},{0,8},{8,16},{16,24},{24,32},{32,40},{40,48},{48,56},{56,6... | collective-permute-start | bytes 6152 | tf_op jit(solution)/shard_map/while/body/eval_jaxpr/ppermute | solution.py:10
  74.2 8.9 %collective-permute-start.4 = (f32[512]{0:T(512)S(1)}, f32[512]{0:T(512)S(1)}, u32[]{:S(2)}, u32[]{:S(2)}) collective-permute-start(f32[512]{0:T(512)S(1)} %copy.23), channel_id=1, source_target_pairs={{248,0},{0,8},{8,16},{16,24},{24,32},{32,40},{40,48},{48,56},{56,6... | collective-permute-start | bytes 6152 | tf_op jit(solution)/shard_map/while/body/eval_jaxpr/ppermute | solution.py:10
  74.3 8.8 %collective-permute-start = (bf16[512,128]{1,0:T(8,128)(2,1)S(1)}, bf16[512,128]{1,0:T(8,128)(2,1)S(1)}, u32[]{:S(2)}, u32[]{:S(2)}) collective-permute-start(bf16[512,128]{1,0:T(8,128)(2,1)S(1)} %copy.19), channel_id=1, source_target_pairs={{248,0},{0,8},{8,16},{16,24},{24,32},{32,40},{40,48},{48,56},{56,6... | collective-permute-start | bytes 393224 | tf_op jit(solution)/shard_map/while/body/eval_jaxpr/ppermute | solution.py:10
  74.5 8.7 %collective-permute-start.1 = (bf16[512,128]{1,0:T(8,128)(2,1)S(1)}, bf16[512,128]{1,0:T(8,128)(2,1)S(1)}, u32[]{:S(2)}, u32[]{:S(2)}) collective-permute-start(bf16[512,128]{1,0:T(8,128)(2,1)S(1)} %copy.20), channel_id=1, source_target_pairs={{248,0},{0,8},{8,16},{16,24},{24,32},{32,40},{40,48},{48,56},{56,6... | collective-permute-start | bytes 393224 | tf_op jit(solution)/shard_map/while/body/eval_jaxpr/ppermute | solution.py:10
  85.6 10.4 %collective-permute-start.3 = (f32[512]{0:T(512)S(1)}, f32[512]{0:T(512)S(1)}, u32[]{:S(2)}, u32[]{:S(2)}) collective-permute-start(f32[512]{0:T(512)S(1)} %copy.22), channel_id=1, source_target_pairs={{248,0},{0,8},{8,16},{16,24},{24,32},{32,40},{40,48},{48,56},{56,6... | collective-permute-start | bytes 6152 | tf_op jit(solution)/shard_map/while/body/eval_jaxpr/ppermute | solution.py:10
  98.6 11.0 %collective-permute-start.3 = (f32[512]{0:T(512)S(1)}, f32[512]{0:T(512)S(1)}, u32[]{:S(2)}, u32[]{:S(2)}) collective-permute-start(f32[512]{0:T(512)S(1)} %copy.22), channel_id=1, source_target_pairs={{248,0},{0,8},{8,16},{16,24},{24,32},{32,40},{40,48},{48,56},{56,6... | collective-permute-start | bytes 6152 | tf_op jit(solution)/shard_map/while/body/eval_jaxpr/ppermute | solution.py:10
  112.1 10.4 %collective-permute-start.3 = (f32[512]{0:T(512)S(1)}, f32[512]{0:T(512)S(1)}, u32[]{:S(2)}, u32[]{:S(2)}) collective-permute-start(f32[512]{0:T(512)S(1)} %copy.22), channel_id=1, source_target_pairs={{248,0},{0,8},{8,16},{16,24},{24,32},{32,40},{40,48},{48,56},{56,6... | collective-permute-start | bytes 6152 | tf_op jit(solution)/shard_map/while/body/eval_jaxpr/ppermute | solution.py:10
  125.1 11.5 %collective-permute-start.3 = (f32[512]{0:T(512)S(1)}, f32[512]{0:T(512)S(1)}, u32[]{:S(2)}, u32[]{:S(2)}) collective-permute-start(f32[512]{0:T(512)S(1)} %copy.22), channel_id=1, source_target_pairs={{248,0},{0,8},{8,16},{16,24},{24,32},{32,40},{40,48},{48,56},{56,6... | collective-permute-start | bytes 6152 | tf_op jit(solution)/shard_map/while/body/eval_jaxpr/ppermute | solution.py:10
  127.6 9.1 %collective-permute-start.4 = (f32[512]{0:T(512)S(1)}, f32[512]{0:T(512)S(1)}, u32[]{:S(2)}, u32[]{:S(2)}) collective-permute-start(f32[512]{0:T(512)S(1)} %copy.23), channel_id=1, source_target_pairs={{248,0},{0,8},{8,16},{16,24},{24,32},{32,40},{40,48},{48,56},{56,6... | collective-permute-start | bytes 6152 | tf_op jit(solution)/shard_map/while/body/eval_jaxpr/ppermute | solution.py:10
  127.7 9.0 %collective-permute-start = (bf16[512,128]{1,0:T(8,128)(2,1)S(1)}, bf16[512,128]{1,0:T(8,128)(2,1)S(1)}, u32[]{:S(2)}, u32[]{:S(2)}) collective-permute-start(bf16[512,128]{1,0:T(8,128)(2,1)S(1)} %copy.19), channel_id=1, source_target_pairs={{248,0},{0,8},{8,16},{16,24},{24,32},{32,40},{40,48},{48,56},{56,6... | collective-permute-start | bytes 393224 | tf_op jit(solution)/shard_map/while/body/eval_jaxpr/ppermute | solution.py:10
  127.8 8.9 %collective-permute-start.1 = (bf16[512,128]{1,0:T(8,128)(2,1)S(1)}, bf16[512,128]{1,0:T(8,128)(2,1)S(1)}, u32[]{:S(2)}, u32[]{:S(2)}) collective-permute-start(bf16[512,128]{1,0:T(8,128)(2,1)S(1)} %copy.20), channel_id=1, source_target_pairs={{248,0},{0,8},{8,16},{16,24},{24,32},{32,40},{40,48},{48,56},{56,6... | collective-permute-start | bytes 393224 | tf_op jit(solution)/shard_map/while/body/eval_jaxpr/ppermute | solution.py:10
  139.2 10.4 %collective-permute-start.3 = (f32[512]{0:T(512)S(1)}, f32[512]{0:T(512)S(1)}, u32[]{:S(2)}, u32[]{:S(2)}) collective-permute-start(f32[512]{0:T(512)S(1)} %copy.22), channel_id=1, source_target_pairs={{248,0},{0,8},{8,16},{16,24},{24,32},{32,40},{40,48},{48,56},{56,6... | collective-permute-start | bytes 6152 | tf_op jit(solution)/shard_map/while/body/eval_jaxpr/ppermute | solution.py:10
  152.1 11.3 %collective-permute-start.3 = (f32[512]{0:T(512)S(1)}, f32[512]{0:T(512)S(1)}, u32[]{:S(2)}, u32[]{:S(2)}) collective-permute-start(f32[512]{0:T(512)S(1)} %copy.22), channel_id=1, source_target_pairs={{248,0},{0,8},{8,16},{16,24},{24,32},{32,40},{40,48},{48,56},{56,6... | collective-permute-start | bytes 6152 | tf_op jit(solution)/shard_map/while/body/eval_jaxpr/ppermute | solution.py:10
  154.6 8.9 %collective-permute-start.4 = (f32[512]{0:T(512)S(1)}, f32[512]{0:T(512)S(1)}, u32[]{:S(2)}, u32[]{:S(2)}) collective-permute-start(f32[512]{0:T(512)S(1)} %copy.23), channel_id=1, source_target_pairs={{248,0},{0,8},{8,16},{16,24},{24,32},{32,40},{40,48},{48,56},{56,6... | collective-permute-start | bytes 6152 | tf_op jit(solution)/shard_map/while/body/eval_jaxpr/ppermute | solution.py:10
  154.7 8.8 %collective-permute-start = (bf16[512,128]{1,0:T(8,128)(2,1)S(1)}, bf16[512,128]{1,0:T(8,128)(2,1)S(1)}, u32[]{:S(2)}, u32[]{:S(2)}) collective-permute-start(bf16[512,128]{1,0:T(8,128)(2,1)S(1)} %copy.19), channel_id=1, source_target_pairs={{248,0},{0,8},{8,16},{16,24},{24,32},{32,40},{40,48},{48,56},{56,6... | collective-permute-start | bytes 393224 | tf_op jit(solution)/shard_map/while/body/eval_jaxpr/ppermute | solution.py:10
  166.0 10.4 %collective-permute-start.3 = (f32[512]{0:T(512)S(1)}, f32[512]{0:T(512)S(1)}, u32[]{:S(2)}, u32[]{:S(2)}) collective-permute-start(f32[512]{0:T(512)S(1)} %copy.22), channel_id=1, source_target_pairs={{248,0},{0,8},{8,16},{16,24},{24,32},{32,40},{40,48},{48,56},{56,6... | collective-permute-start | bytes 6152 | tf_op jit(solution)/shard_map/while/body/eval_jaxpr/ppermute | solution.py:10
  178.9 11.3 %collective-permute-start.3 = (f32[512]{0:T(512)S(1)}, f32[512]{0:T(512)S(1)}, u32[]{:S(2)}, u32[]{:S(2)}) collective-permute-start(f32[512]{0:T(512)S(1)} %copy.22), channel_id=1, source_target_pairs={{248,0},{0,8},{8,16},{16,24},{24,32},{32,40},{40,48},{48,56},{56,6... | collective-permute-start | bytes 6152 | tf_op jit(solution)/shard_map/while/body/eval_jaxpr/ppermute | solution.py:10
  181.4 8.9 %collective-permute-start.4 = (f32[512]{0:T(512)S(1)}, f32[512]{0:T(512)S(1)}, u32[]{:S(2)}, u32[]{:S(2)}) collective-permute-start(f32[512]{0:T(512)S(1)} %copy.23), channel_id=1, source_target_pairs={{248,0},{0,8},{8,16},{16,24},{24,32},{32,40},{40,48},{48,56},{56,6... | collective-permute-start | bytes 6152 | tf_op jit(solution)/shard_map/while/body/eval_jaxpr/ppermute | solution.py:10
  181.5 8.8 %collective-permute-start = (bf16[512,128]{1,0:T(8,128)(2,1)S(1)}, bf16[512,128]{1,0:T(8,128)(2,1)S(1)}, u32[]{:S(2)}, u32[]{:S(2)}) collective-permute-start(bf16[512,128]{1,0:T(8,128)(2,1)S(1)} %copy.19), channel_id=1, source_target_pairs={{248,0},{0,8},{8,16},{16,24},{24,32},{32,40},{40,48},{48,56},{56,6... | collective-permute-start | bytes 393224 | tf_op jit(solution)/shard_map/while/body/eval_jaxpr/ppermute | solution.py:10
  192.8 10.4 %collective-permute-start.3 = (f32[512]{0:T(512)S(1)}, f32[512]{0:T(512)S(1)}, u32[]{:S(2)}, u32[]{:S(2)}) collective-permute-start(f32[512]{0:T(512)S(1)} %copy.22), channel_id=1, source_target_pairs={{248,0},{0,8},{8,16},{16,24},{24,32},{32,40},{40,48},{48,56},{56,6... | collective-permute-start | bytes 6152 | tf_op jit(solution)/shard_map/while/body/eval_jaxpr/ppermute | solution.py:10
  205.8 11.0 %collective-permute-start.3 = (f32[512]{0:T(512)S(1)}, f32[512]{0:T(512)S(1)}, u32[]{:S(2)}, u32[]{:S(2)}) collective-permute-start(f32[512]{0:T(512)S(1)} %copy.22), channel_id=1, source_target_pairs={{248,0},{0,8},{8,16},{16,24},{24,32},{32,40},{40,48},{48,56},{56,6... | collective-permute-start | bytes 6152 | tf_op jit(solution)/shard_map/while/body/eval_jaxpr/ppermute | solution.py:10
  219.3 10.4 %collective-permute-start.3 = (f32[512]{0:T(512)S(1)}, f32[512]{0:T(512)S(1)}, u32[]{:S(2)}, u32[]{:S(2)}) collective-permute-start(f32[512]{0:T(512)S(1)} %copy.22), channel_id=1, source_target_pairs={{248,0},{0,8},{8,16},{16,24},{24,32},{32,40},{40,48},{48,56},{56,6... | collective-permute-start | bytes 6152 | tf_op jit(solution)/shard_map/while/body/eval_jaxpr/ppermute | solution.py:10
  232.3 11.5 %collective-permute-start.3 = (f32[512]{0:T(512)S(1)}, f32[512]{0:T(512)S(1)}, u32[]{:S(2)}, u32[]{:S(2)}) collective-permute-start(f32[512]{0:T(512)S(1)} %copy.22), channel_id=1, source_target_pairs={{248,0},{0,8},{8,16},{16,24},{24,32},{32,40},{40,48},{48,56},{56,6... | collective-permute-start | bytes 6152 | tf_op jit(solution)/shard_map/while/body/eval_jaxpr/ppermute | solution.py:10
  234.8 9.1 %collective-permute-start.4 = (f32[512]{0:T(512)S(1)}, f32[512]{0:T(512)S(1)}, u32[]{:S(2)}, u32[]{:S(2)}) collective-permute-start(f32[512]{0:T(512)S(1)} %copy.23), channel_id=1, source_target_pairs={{248,0},{0,8},{8,16},{16,24},{24,32},{32,40},{40,48},{48,56},{56,6... | collective-permute-start | bytes 6152 | tf_op jit(solution)/shard_map/while/body/eval_jaxpr/ppermute | solution.py:10
  234.9 9.0 %collective-permute-start = (bf16[512,128]{1,0:T(8,128)(2,1)S(1)}, bf16[512,128]{1,0:T(8,128)(2,1)S(1)}, u32[]{:S(2)}, u32[]{:S(2)}) collective-permute-start(bf16[512,128]{1,0:T(8,128)(2,1)S(1)} %copy.19), channel_id=1, source_target_pairs={{248,0},{0,8},{8,16},{16,24},{24,32},{32,40},{40,48},{48,56},{56,6... | collective-permute-start | bytes 393224 | tf_op jit(solution)/shard_map/while/body/eval_jaxpr/ppermute | solution.py:10
  235.0 8.9 %collective-permute-start.1 = (bf16[512,128]{1,0:T(8,128)(2,1)S(1)}, bf16[512,128]{1,0:T(8,128)(2,1)S(1)}, u32[]{:S(2)}, u32[]{:S(2)}) collective-permute-start(bf16[512,128]{1,0:T(8,128)(2,1)S(1)} %copy.20), channel_id=1, source_target_pairs={{248,0},{0,8},{8,16},{16,24},{24,32},{32,40},{40,48},{48,56},{56,6... | collective-permute-start | bytes 393224 | tf_op jit(solution)/shard_map/while/body/eval_jaxpr/ppermute | solution.py:10
  246.4 10.4 %collective-permute-start.3 = (f32[512]{0:T(512)S(1)}, f32[512]{0:T(512)S(1)}, u32[]{:S(2)}, u32[]{:S(2)}) collective-permute-start(f32[512]{0:T(512)S(1)} %copy.22), channel_id=1, source_target_pairs={{248,0},{0,8},{8,16},{16,24},{24,32},{32,40},{40,48},{48,56},{56,6... | collective-permute-start | bytes 6152 | tf_op jit(solution)/shard_map/while/body/eval_jaxpr/ppermute | solution.py:10
  259.3 11.3 %collective-permute-start.3 = (f32[512]{0:T(512)S(1)}, f32[512]{0:T(512)S(1)}, u32[]{:S(2)}, u32[]{:S(2)}) collective-permute-start(f32[512]{0:T(512)S(1)} %copy.22), channel_id=1, source_target_pairs={{248,0},{0,8},{8,16},{16,24},{24,32},{32,40},{40,48},{48,56},{56,6... | collective-permute-start | bytes 6152 | tf_op jit(solution)/shard_map/while/body/eval_jaxpr/ppermute | solution.py:10
  261.8 8.9 %collective-permute-start.4 = (f32[512]{0:T(512)S(1)}, f32[512]{0:T(512)S(1)}, u32[]{:S(2)}, u32[]{:S(2)}) collective-permute-start(f32[512]{0:T(512)S(1)} %copy.23), channel_id=1, source_target_pairs={{248,0},{0,8},{8,16},{16,24},{24,32},{32,40},{40,48},{48,56},{56,6... | collective-permute-start | bytes 6152 | tf_op jit(solution)/shard_map/while/body/eval_jaxpr/ppermute | solution.py:10
  261.9 8.8 %collective-permute-start = (bf16[512,128]{1,0:T(8,128)(2,1)S(1)}, bf16[512,128]{1,0:T(8,128)(2,1)S(1)}, u32[]{:S(2)}, u32[]{:S(2)}) collective-permute-start(bf16[512,128]{1,0:T(8,128)(2,1)S(1)} %copy.19), channel_id=1, source_target_pairs={{248,0},{0,8},{8,16},{16,24},{24,32},{32,40},{40,48},{48,56},{56,6... | collective-permute-start | bytes 393224 | tf_op jit(solution)/shard_map/while/body/eval_jaxpr/ppermute | solution.py:10
  273.2 10.4 %collective-permute-start.3 = (f32[512]{0:T(512)S(1)}, f32[512]{0:T(512)S(1)}, u32[]{:S(2)}, u32[]{:S(2)}) collective-permute-start(f32[512]{0:T(512)S(1)} %copy.22), channel_id=1, source_target_pairs={{248,0},{0,8},{8,16},{16,24},{24,32},{32,40},{40,48},{48,56},{56,6... | collective-permute-start | bytes 6152 | tf_op jit(solution)/shard_map/while/body/eval_jaxpr/ppermute | solution.py:10
  286.1 11.3 %collective-permute-start.3 = (f32[512]{0:T(512)S(1)}, f32[512]{0:T(512)S(1)}, u32[]{:S(2)}, u32[]{:S(2)}) collective-permute-start(f32[512]{0:T(512)S(1)} %copy.22), channel_id=1, source_target_pairs={{248,0},{0,8},{8,16},{16,24},{24,32},{32,40},{40,48},{48,56},{56,6... | collective-permute-start | bytes 6152 | tf_op jit(solution)/shard_map/while/body/eval_jaxpr/ppermute | solution.py:10
  288.6 8.9 %collective-permute-start.4 = (f32[512]{0:T(512)S(1)}, f32[512]{0:T(512)S(1)}, u32[]{:S(2)}, u32[]{:S(2)}) collective-permute-start(f32[512]{0:T(512)S(1)} %copy.23), channel_id=1, source_target_pairs={{248,0},{0,8},{8,16},{16,24},{24,32},{32,40},{40,48},{48,56},{56,6... | collective-permute-start | bytes 6152 | tf_op jit(solution)/shard_map/while/body/eval_jaxpr/ppermute | solution.py:10
  288.7 8.8 %collective-permute-start = (bf16[512,128]{1,0:T(8,128)(2,1)S(1)}, bf16[512,128]{1,0:T(8,128)(2,1)S(1)}, u32[]{:S(2)}, u32[]{:S(2)}) collective-permute-start(bf16[512,128]{1,0:T(8,128)(2,1)S(1)} %copy.19), channel_id=1, source_target_pairs={{248,0},{0,8},{8,16},{16,24},{24,32},{32,40},{40,48},{48,56},{56,6... | collective-permute-start | bytes 393224 | tf_op jit(solution)/shard_map/while/body/eval_jaxpr/ppermute | solution.py:10
  300.0 10.4 %collective-permute-start.3 = (f32[512]{0:T(512)S(1)}, f32[512]{0:T(512)S(1)}, u32[]{:S(2)}, u32[]{:S(2)}) collective-permute-start(f32[512]{0:T(512)S(1)} %copy.22), channel_id=1, source_target_pairs={{248,0},{0,8},{8,16},{16,24},{24,32},{32,40},{40,48},{48,56},{56,6... | collective-permute-start | bytes 6152 | tf_op jit(solution)/shard_map/while/body/eval_jaxpr/ppermute | solution.py:10
  313.0 11.0 %collective-permute-start.3 = (f32[512]{0:T(512)S(1)}, f32[512]{0:T(512)S(1)}, u32[]{:S(2)}, u32[]{:S(2)}) collective-permute-start(f32[512]{0:T(512)S(1)} %copy.22), channel_id=1, source_target_pairs={{248,0},{0,8},{8,16},{16,24},{24,32},{32,40},{40,48},{48,56},{56,6... | collective-permute-start | bytes 6152 | tf_op jit(solution)/shard_map/while/body/eval_jaxpr/ppermute | solution.py:10
  326.5 10.4 %collective-permute-start.3 = (f32[512]{0:T(512)S(1)}, f32[512]{0:T(512)S(1)}, u32[]{:S(2)}, u32[]{:S(2)}) collective-permute-start(f32[512]{0:T(512)S(1)} %copy.22), channel_id=1, source_target_pairs={{248,0},{0,8},{8,16},{16,24},{24,32},{32,40},{40,48},{48,56},{56,6... | collective-permute-start | bytes 6152 | tf_op jit(solution)/shard_map/while/body/eval_jaxpr/ppermute | solution.py:10
  339.5 11.5 %collective-permute-start.3 = (f32[512]{0:T(512)S(1)}, f32[512]{0:T(512)S(1)}, u32[]{:S(2)}, u32[]{:S(2)}) collective-permute-start(f32[512]{0:T(512)S(1)} %copy.22), channel_id=1, source_target_pairs={{248,0},{0,8},{8,16},{16,24},{24,32},{32,40},{40,48},{48,56},{56,6... | collective-permute-start | bytes 6152 | tf_op jit(solution)/shard_map/while/body/eval_jaxpr/ppermute | solution.py:10
  342.0 9.1 %collective-permute-start.4 = (f32[512]{0:T(512)S(1)}, f32[512]{0:T(512)S(1)}, u32[]{:S(2)}, u32[]{:S(2)}) collective-permute-start(f32[512]{0:T(512)S(1)} %copy.23), channel_id=1, source_target_pairs={{248,0},{0,8},{8,16},{16,24},{24,32},{32,40},{40,48},{48,56},{56,6... | collective-permute-start | bytes 6152 | tf_op jit(solution)/shard_map/while/body/eval_jaxpr/ppermute | solution.py:10
  342.1 9.0 %collective-permute-start = (bf16[512,128]{1,0:T(8,128)(2,1)S(1)}, bf16[512,128]{1,0:T(8,128)(2,1)S(1)}, u32[]{:S(2)}, u32[]{:S(2)}) collective-permute-start(bf16[512,128]{1,0:T(8,128)(2,1)S(1)} %copy.19), channel_id=1, source_target_pairs={{248,0},{0,8},{8,16},{16,24},{24,32},{32,40},{40,48},{48,56},{56,6... | collective-permute-start | bytes 393224 | tf_op jit(solution)/shard_map/while/body/eval_jaxpr/ppermute | solution.py:10
  342.2 8.9 %collective-permute-start.1 = (bf16[512,128]{1,0:T(8,128)(2,1)S(1)}, bf16[512,128]{1,0:T(8,128)(2,1)S(1)}, u32[]{:S(2)}, u32[]{:S(2)}) collective-permute-start(bf16[512,128]{1,0:T(8,128)(2,1)S(1)} %copy.20), channel_id=1, source_target_pairs={{248,0},{0,8},{8,16},{16,24},{24,32},{32,40},{40,48},{48,56},{56,6... | collective-permute-start | bytes 393224 | tf_op jit(solution)/shard_map/while/body/eval_jaxpr/ppermute | solution.py:10
  353.5 10.4 %collective-permute-start.3 = (f32[512]{0:T(512)S(1)}, f32[512]{0:T(512)S(1)}, u32[]{:S(2)}, u32[]{:S(2)}) collective-permute-start(f32[512]{0:T(512)S(1)} %copy.22), channel_id=1, source_target_pairs={{248,0},{0,8},{8,16},{16,24},{24,32},{32,40},{40,48},{48,56},{56,6... | collective-permute-start | bytes 6152 | tf_op jit(solution)/shard_map/while/body/eval_jaxpr/ppermute | solution.py:10
  366.5 11.3 %collective-permute-start.3 = (f32[512]{0:T(512)S(1)}, f32[512]{0:T(512)S(1)}, u32[]{:S(2)}, u32[]{:S(2)}) collective-permute-start(f32[512]{0:T(512)S(1)} %copy.22), channel_id=1, source_target_pairs={{248,0},{0,8},{8,16},{16,24},{24,32},{32,40},{40,48},{48,56},{56,6... | collective-permute-start | bytes 6152 | tf_op jit(solution)/shard_map/while/body/eval_jaxpr/ppermute | solution.py:10
  369.0 8.9 %collective-permute-start.4 = (f32[512]{0:T(512)S(1)}, f32[512]{0:T(512)S(1)}, u32[]{:S(2)}, u32[]{:S(2)}) collective-permute-start(f32[512]{0:T(512)S(1)} %copy.23), channel_id=1, source_target_pairs={{248,0},{0,8},{8,16},{16,24},{24,32},{32,40},{40,48},{48,56},{56,6... | collective-permute-start | bytes 6152 | tf_op jit(solution)/shard_map/while/body/eval_jaxpr/ppermute | solution.py:10
  369.1 8.8 %collective-permute-start = (bf16[512,128]{1,0:T(8,128)(2,1)S(1)}, bf16[512,128]{1,0:T(8,128)(2,1)S(1)}, u32[]{:S(2)}, u32[]{:S(2)}) collective-permute-start(bf16[512,128]{1,0:T(8,128)(2,1)S(1)} %copy.19), channel_id=1, source_target_pairs={{248,0},{0,8},{8,16},{16,24},{24,32},{32,40},{40,48},{48,56},{56,6... | collective-permute-start | bytes 393224 | tf_op jit(solution)/shard_map/while/body/eval_jaxpr/ppermute | solution.py:10
  380.4 10.4 %collective-permute-start.3 = (f32[512]{0:T(512)S(1)}, f32[512]{0:T(512)S(1)}, u32[]{:S(2)}, u32[]{:S(2)}) collective-permute-start(f32[512]{0:T(512)S(1)} %copy.22), channel_id=1, source_target_pairs={{248,0},{0,8},{8,16},{16,24},{24,32},{32,40},{40,48},{48,56},{56,6... | collective-permute-start | bytes 6152 | tf_op jit(solution)/shard_map/while/body/eval_jaxpr/ppermute | solution.py:10
  393.3 11.3 %collective-permute-start.3 = (f32[512]{0:T(512)S(1)}, f32[512]{0:T(512)S(1)}, u32[]{:S(2)}, u32[]{:S(2)}) collective-permute-start(f32[512]{0:T(512)S(1)} %copy.22), channel_id=1, source_target_pairs={{248,0},{0,8},{8,16},{16,24},{24,32},{32,40},{40,48},{48,56},{56,6... | collective-permute-start | bytes 6152 | tf_op jit(solution)/shard_map/while/body/eval_jaxpr/ppermute | solution.py:10
  395.8 8.9 %collective-permute-start.4 = (f32[512]{0:T(512)S(1)}, f32[512]{0:T(512)S(1)}, u32[]{:S(2)}, u32[]{:S(2)}) collective-permute-start(f32[512]{0:T(512)S(1)} %copy.23), channel_id=1, source_target_pairs={{248,0},{0,8},{8,16},{16,24},{24,32},{32,40},{40,48},{48,56},{56,6... | collective-permute-start | bytes 6152 | tf_op jit(solution)/shard_map/while/body/eval_jaxpr/ppermute | solution.py:10
  395.9 8.8 %collective-permute-start = (bf16[512,128]{1,0:T(8,128)(2,1)S(1)}, bf16[512,128]{1,0:T(8,128)(2,1)S(1)}, u32[]{:S(2)}, u32[]{:S(2)}) collective-permute-start(bf16[512,128]{1,0:T(8,128)(2,1)S(1)} %copy.19), channel_id=1, source_target_pairs={{248,0},{0,8},{8,16},{16,24},{24,32},{32,40},{40,48},{48,56},{56,6... | collective-permute-start | bytes 393224 | tf_op jit(solution)/shard_map/while/body/eval_jaxpr/ppermute | solution.py:10
  407.2 10.4 %collective-permute-start.3 = (f32[512]{0:T(512)S(1)}, f32[512]{0:T(512)S(1)}, u32[]{:S(2)}, u32[]{:S(2)}) collective-permute-start(f32[512]{0:T(512)S(1)} %copy.22), channel_id=1, source_target_pairs={{248,0},{0,8},{8,16},{16,24},{24,32},{32,40},{40,48},{48,56},{56,6... | collective-permute-start | bytes 6152 | tf_op jit(solution)/shard_map/while/body/eval_jaxpr/ppermute | solution.py:10
  420.1 11.0 %collective-permute-start.3 = (f32[512]{0:T(512)S(1)}, f32[512]{0:T(512)S(1)}, u32[]{:S(2)}, u32[]{:S(2)}) collective-permute-start(f32[512]{0:T(512)S(1)} %copy.22), channel_id=1, source_target_pairs={{248,0},{0,8},{8,16},{16,24},{24,32},{32,40},{40,48},{48,56},{56,6... | collective-permute-start | bytes 6152 | tf_op jit(solution)/shard_map/while/body/eval_jaxpr/ppermute | solution.py:10
  434.5 27.9 %all-to-all-start = ((f32[8,64,256]{2,1,0:T(8,128)}), f32[8,64,256]{2,1,0:T(8,128)S(1)}, u32[]{:S(2)}, u32[]{:S(2)}) async-start(f32[8,64,256]{2,1,0:T(8,128)} %bitcast.7), calls=%async_computation | async-start | bytes 1048576 | tf_op jit(solution)/shard_map/all_to_all | solution.py:21
  (103 other events, 767.8 us)
where the time goes:
time: 465 us; the launch traced here: 464 us
  starting transfers between devices  240 us (52%)
  waiting for transfers between devices  98.8 us (21%)
  matrix products  56 us (12%)
  loops' own time  41.9 us (9%)
  local copies, waits for them, and re-layouts  24 us (5%)
    ppermute x160, starting transfers between devices, passed_along(): return lax.ppermute(block, axis, route)  231 us
    ppermute x160, waiting for transfers between devices, passed_along(): return lax.ppermute(block, axis, route)  80 us
    another operation x1, loops' own time, on_device(): final = lax.fori_loop(0, devices, turn, start)  41.9 us
    dot_general x64, matrix products, outer(): lax.dot_general(left, right, (((0,), (0,)), ((), ())), preferred_element_...  24.6 us
    dot_general x64, matrix products, inner(): lax.dot_general(left, right, (((1,), (1,)), ((), ())), preferred_element_...  21.9 us
    dynamic_slice x33, local copies, waits for them, and re-layouts, place(): lax.dynamic_index_in_dim(block_order, block, 0, keepdims=False) * half  19.4 us
    all_to_all x1, waiting for transfers between devices, sum_at_owner(): lax.all_to_all(pieces, axis, split_axis=0, concat_axis=0, tiled=True)  18.9 us
    dot_general x32, matrix products, tile_grads(): grad_q = jnp.dot(dscores, key, preferred_element_type=jnp.float32) * scale  9.47 us
  transfers between devices with their start and end apart: 161, of which 33 were waited for; matrix products, arithmetic and copies ran while one was open for 16% of the time, Pallas kernels for 0%

commit v1 on v0

v1 whole, which is shorter than its diff:
```python
import jax
import jax.numpy as jnp
from jax import lax
from jax.experimental import pallas as pl
from jax.experimental.pallas import tpu as pltpu
from jax.sharding import PartitionSpec as P

F32 = jnp.float32
BF16 = jnp.bfloat16
MESH = pl.DeviceIdType.MESH
LOG2E = 1.4426950408889634
DEAD = 1.0e9
X, Z, C, Y = 4, 4, 2, 4
RING = 8


def dot(left, right, left_dim, right_dim):
    return lax.dot_general(
        left, right, (((left_dim,), (right_dim,)), ((), ())), preferred_element_type=F32
    )


def kernel(
    q_hbm, k_hbm, v_hbm, o_hbm, g_hbm, l_hbm, order,
    dq_out, dk_out, dv_out,
    qb, gb, sb, kb, vb, ob, lb,
    dq_acc, dk_acc, dv_acc, core_in, x_out, x_in,
    y_out, y_own, y_in, z_out, z_own, z_in,
    load_sem, send_sem, q_sem, g_sem, s_sem, k_sem, v_sem, core_sem, x_sem, y_sem, z_sem,
):
    rows, feat = k_hbm.shape
    half = rows // 2
    scale = feat ** -0.5
    blk = lax.axis_index("blk")
    head = lax.axis_index("head")
    core = blk % C
    zlo = (blk // C) % Z
    x = blk // (C * Z)
    zhi = head % 2
    y = head // 2
    ring = zhi * Z + zlo

    def at(dx=0, dc=0):
        return {"blk": (((x + dx) % X) * Z + zlo) * C + (core + dc) % C, "head": head}

    def at_y(dy):
        return {"blk": blk, "head": ((y + dy) % Y) * 2 + zhi}

    def at_ring(dz):
        there = (ring + dz) % RING
        return {"blk": (x * Z + there % Z) * C + core, "head": y * 2 + there // Z}

    greeted = (
        [at(dc=1)] + [at(dx=i) for i in (1, 2, 3)] + [at_y(i) for i in (1, 2, 3)]
        + [at_ring(i) for i in range(1, RING)]
    )
    barrier = pltpu.get_barrier_semaphore()
    for device in greeted:
        pl.semaphore_signal(barrier, inc=1, device_id=device, device_id_type=MESH)

    loads = []
    own = pl.ds(0, rows)
    for i, (src, dst) in enumerate((
        (g_hbm.at[0], gb.at[0, own]), (o_hbm.at[0], ob), (l_hbm, lb),
        (q_hbm.at[0], qb.at[0, own]), (k_hbm, kb.at[0]), (v_hbm, vb.at[0]),
    )):
        loads.append(pltpu.make_async_copy(src, dst, load_sem.at[i]))
        loads[-1].start()

    sends = []

    def remote(src, dst, recv, device):
        copy = pltpu.make_async_remote_copy(
            src_ref=src, dst_ref=dst, send_sem=send_sem.at[len(sends)], recv_sem=recv,
            device_id=device, device_id_type=MESH,
        )
        sends.append(copy)
        return copy

    def landing(dst, recv):
        return pltpu.make_async_remote_copy(
            src_ref=dst, dst_ref=dst, send_sem=send_sem.at[0], recv_sem=recv,
            device_id=at(dc=1), device_id_type=MESH,
        )

    def slot(buf, s):
        return buf.at[s // 2, pl.ds((s % 2) * rows, rows)]

    def stat(s):
        return sb.at[s // 2, :, pl.ds((s % 2) * rows, rows)]

    def pass_slot(src, dst, device):
        return [
            remote(slot(qb, src), slot(qb, dst), q_sem.at[dst], device),
            remote(slot(gb, src), slot(gb, dst), g_sem.at[dst], device),
            remote(stat(src), stat(dst), s_sem.at[dst], device),
        ]

    def wait_slot(s):
        landing(slot(qb, s), q_sem.at[s]).wait_recv()
        landing(slot(gb, s), g_sem.at[s]).wait_recv()
        landing(stat(s), s_sem.at[s]).wait_recv()

    to_core = pass_slot(0, 1, at(dc=1))
    to_right = pass_slot(0, 3, at(dx=1))
    to_left = pass_slot(0, 2, at(dx=3))
    keys_out = [
        remote(kb.at[0], kb.at[2], k_sem.at[2], at_ring(1)),
        remote(kb.at[0], kb.at[1], k_sem.at[1], at_ring(7)),
        remote(vb.at[0], vb.at[2], v_sem.at[2], at_ring(1)),
        remote(vb.at[0], vb.at[1], v_sem.at[1], at_ring(7)),
    ]
    forward = pass_slot(2, 4, at(dc=1)) + pass_slot(3, 5, at(dc=1))
    relay_x = [
        remote(slot(qb, 2), slot(qb, 6), q_sem.at[6], at(dx=3)),
        remote(slot(gb, 3), slot(gb, 6), g_sem.at[6], at(dx=1)),
        remote(stat(2), stat(6), s_sem.at[6], at(dx=3)),
    ]
    relay_z = [
        remote(kb.at[1], kb.at[3], k_sem.at[3], at_ring(7)),
        remote(vb.at[2], vb.at[3], v_sem.at[3], at_ring(1)),
    ]
    forward_far = pass_slot(6, 7, at(dc=1))
    core_pairs = {7: 6, 4: 2, 5: 3, 1: 0}
    core_index = {7: 0, 4: 1, 5: 2, 1: 3}
    dq_core = {
        s: remote(dq_acc.at[s], core_in.at[i], core_sem.at[i], at(dc=1))
        for s, i in core_index.items()
    }
    dq_x = {i: remote(x_out.at[i - 1], x_in.at[i - 1], x_sem.at[i - 1], at(dx=i)) for i in (1, 2, 3)}
    kv_y = {
        (r, i): remote(y_out.at[r, (y + i) % Y], y_in.at[r, i - 1], y_sem.at[r, i - 1], at_y(i))
        for r in range(Z) for i in (1, 2, 3)
    }
    turn_of = (0, 1, 3, 2)
    kv_z = {}
    for r in range(Z):
        for i in (turn_of[r], turn_of[r] + Z):
            if i:
                there = (ring + i) % RING
                kv_z[r, i] = remote(
                    z_out.at[r, there // Z], z_in.at[i - 1], z_sem.at[i - 1], at_ring(i)
                )

    def start(copies):
        for copy in copies:
            copy.start()

    loads[0].wait()
    loads[1].wait()
    loads[2].wait()
    delta = jnp.sum(jnp.transpose(gb[0, own].astype(F32) * ob[...].astype(F32)), axis=0, keepdims=True)
    sb[0, 0:1, own] = lb[...] * LOG2E
    sb[0, 1:2, own] = delta
    for i in (3, 4, 5):
        loads[i].wait()
    pl.semaphore_wait(barrier, len(greeted))

    start(to_core[:2])
    start([to_right[0], to_left[0], to_right[1], to_left[1]])
    start(keys_out)

    dq_acc[...] = jnp.zeros_like(dq_acc)
    dk_acc[...] = jnp.zeros_like(dk_acc)
    dv_acc[...] = jnp.zeros_like(dv_acc)
    start([to_core[2], to_right[2], to_left[2]])

    def chunk_blocks(dx, dc, dz):
        c = ((x + dx) % X * Z + (zlo + dz) % Z) * C + (core + dc) % C
        return order[2 * c], order[2 * c + 1]

    def grads(keys, vals, q_rows, g_rows, probs, d_row):
        dprobs = dot(vals, g_rows, 1, 1)
        dscores = (probs * (dprobs - d_row)).astype(BF16)
        dv_acc[...] += dot(probs.astype(BF16), g_rows, 1, 0)
        dk_acc[...] += dot(dscores, q_rows, 1, 0)
        return dot(keys, dscores, 0, 0)

    def biased(l_row, q_blocks, k_block):
        parts = []
        for i, q_block in enumerate(q_blocks):
            dead = jnp.where(q_block > k_block, 0.0, DEAD)
            parts.append(l_row[:, i * half : (i + 1) * half] + dead)
        return jnp.concatenate(parts, axis=1)

    def tile(r, p, first, count, q_blocks, k_blocks):
        cols = pl.ds(first * rows, count * rows)
        keys, vals = kb[r], vb[r]
        q_rows, g_rows = qb[p, cols], gb[p, cols]
        l_row, d_row = sb[p, 0:1, cols], sb[p, 1:2, cols]
        lows = jnp.stack([biased(l_row, q_blocks, b) for b in k_blocks])
        scores = dot(keys, q_rows, 1, 1).reshape(2, half, count * rows)
        probs = jnp.exp2(scores * (scale * LOG2E) - lows).reshape(rows, count * rows)
        part = grads(keys, vals, q_rows, g_rows, probs, d_row)
        for i in range(count):
            dq_acc[2 * p + first + i] += part[:, i * rows : (i + 1) * rows]

    own_blocks = chunk_blocks(0, 0, 0)
    q_rows, g_rows = qb[0, own], gb[0, own]
    at_row = lax.broadcasted_iota(jnp.int32, (rows, rows), 0)
    at_col = lax.broadcasted_iota(jnp.int32, (rows, rows), 1)
    k_pos = jnp.where(at_row < half, own_blocks[0], own_blocks[1]) * half + at_row % half
    q_pos = jnp.where(at_col < half, own_blocks[0], own_blocks[1]) * half + at_col % half
    scores = dot(kb[0], q_rows, 1, 1)
    probs = jnp.where(
        q_pos >= k_pos, jnp.exp2(scores * (scale * LOG2E) - sb[0, 0:1, own]), 0.0
    )
    dq_acc[0] += grads(kb[0], vb[0], q_rows, g_rows, probs, sb[0, 1:2, own])

    wait_slot(1)
    tile(0, 0, 1, 1, chunk_blocks(0, 1, 0), own_blocks)

    quarter = rows // Y
    eighth = quarter // 2

    def stage_row(r):
        y_out[r, :, :, :feat] = dk_acc[...].astype(BF16).reshape(Y, quarter, feat)
        y_out[r, :, :, feat:] = dv_acc[...].astype(BF16).reshape(Y, quarter, feat)
        mine = pl.ds(y * quarter, quarter)
        y_own[r, :, :feat] = dk_acc[mine]
        y_own[r, :, feat:] = dv_acc[mine]
        dk_acc[...] = jnp.zeros_like(dk_acc)
        dv_acc[...] = jnp.zeros_like(dv_acc)

    def sum_y(r):
        total = y_own[r]
        for i in range(Y - 1):
            landing(y_in.at[r, i], y_sem.at[r, i]).wait_recv()
            total = total + y_in[r, i].astype(F32)
        total = total.reshape(2, eighth, 2 * feat)
        z_out[r] = total.astype(BF16)
        if r == 0:
            y_own[0] = total.reshape(quarter, 2 * feat)
            z_own[...] = y_own[0, pl.ds(zhi * eighth, eighth)]

    def send_y(r):
        start([kv_y[r, i] for i in (2, 1, 3)])

    def send_z(r):
        start([copy for (row, _), copy in kv_z.items() if row == r])

    def join_core(s, index):
        i = core_index[s]
        landing(core_in.at[i], core_sem.at[i]).wait_recv()
        x_out[index] = (dq_acc[core_pairs[s]] + core_in[i]).astype(BF16)

    def step(t, carry):
        r = t // 4
        p = t % 4 + (r // 3) * (3 - 2 * (t % 4))

        @pl.when(t == 1)
        def _():
            wait_slot(2)
            wait_slot(3)
            start(forward)
            start(relay_x)

        @pl.when(t == 2)
        def _():
            for i in (1, 2):
                landing(kb.at[i], k_sem.at[i]).wait_recv()
                landing(vb.at[i], v_sem.at[i]).wait_recv()
            start(relay_z)
            wait_slot(4)
            wait_slot(5)

        @pl.when(t == 3)
        def _():
            wait_slot(6)
            start(forward_far)
            wait_slot(7)

        @pl.when(t == 12)
        def _():
            landing(kb.at[3], k_sem.at[3]).wait_recv()
            landing(vb.at[3], v_sem.at[3]).wait_recv()

        near = (p + 1) // 2
        q_blocks = chunk_blocks(near, p // 2 - p // 3, 0) + chunk_blocks(
            4 - near, 1 - p % 2 + p // 3, 0
        )
        k_blocks = chunk_blocks(0, 0, r + r // 2 - 2 * (r // 3))
        tile(r, p, 0, 2, q_blocks, k_blocks)

        for r_done in range(3):
            @pl.when(t == 4 * r_done + 4)
            def _():
                send_y(r_done)
                if r_done >= 1:
                    send_z(r_done - 1)

        for r_done in range(4):
            @pl.when(t == 4 * r_done + 3)
            def _():
                if r_done >= 1:
                    sum_y(r_done - 1)
                stage_row(r_done)

        @pl.when(t == 12)
        def _():
            dq_core[7].start()

        @pl.when(t == 13)
        def _():
            dq_core[4].start()
            dq_core[5].start()
            join_core(7, 1)

        @pl.when(t == 14)
        def _():
            dq_x[2].start()
            join_core(4, 0)
            join_core(5, 2)

        @pl.when(t == 15)
        def _():
            dq_x[1].start()
            dq_x[3].start()
            dq_core[1].start()

        return carry

    lax.fori_loop(1, 16, step, 0)

    send_y(3)
    send_z(2)
    landing(core_in.at[3], core_sem.at[3]).wait_recv()
    total = dq_acc[0] + core_in[3]
    for i in range(X - 1):
        landing(x_in.at[i], x_sem.at[i]).wait_recv()
        total = total + x_in[i].astype(F32)
    dq_out[0] = jnp.transpose(total * scale)
    sum_y(3)
    send_z(3)
    total = z_own[...]
    for i in (4, 1, 5, 3, 7, 2, 6):
        landing(z_in.at[i - 1], z_sem.at[i - 1]).wait_recv()
        total = total + z_in[i - 1].astype(F32)
    dk_out[...] = total[:, :feat] * scale
    dv_out[...] = total[:, feat:]
    for copy in sends:
        copy.wait_send()


def on_device(query, key, value, output, out_grad, lse, block_order):
    rows, feat = key.shape
    quarter, eighth = rows // Y, rows // RING
    any_space = pl.BlockSpec(memory_space=pl.ANY)
    vmem = pl.BlockSpec(memory_space=pltpu.VMEM)
    dma = pltpu.SemaphoreType.DMA
    return pl.pallas_call(
        kernel,
        out_shape=(
            jax.ShapeDtypeStruct((1, rows, feat), F32),
            jax.ShapeDtypeStruct((eighth, feat), F32),
            jax.ShapeDtypeStruct((eighth, feat), F32),
        ),
        in_specs=[any_space] * 6 + [pl.BlockSpec(memory_space=pltpu.SMEM)],
        out_specs=(vmem, vmem, vmem),
        scratch_shapes=[
            pltpu.VMEM((4, 2 * rows, feat), BF16),
            pltpu.VMEM((4, 2 * rows, feat), BF16),
            pltpu.VMEM((4, 2, 2 * rows), F32),
            pltpu.VMEM((Z, rows, feat), BF16),
            pltpu.VMEM((Z, rows, feat), BF16),
            pltpu.VMEM((rows, feat), BF16),
            pltpu.VMEM((1, rows), F32),
            pltpu.VMEM((8, feat, rows), F32),
            pltpu.VMEM((rows, feat), F32),
            pltpu.VMEM((rows, feat), F32),
            pltpu.VMEM((4, feat, rows), F32),
            pltpu.VMEM((X - 1, feat, rows), BF16),
            pltpu.VMEM((X - 1, feat, rows), BF16),
            pltpu.VMEM((Z, Y, quarter, 2 * feat), BF16),
            pltpu.VMEM((Z, quarter, 2 * feat), F32),
            pltpu.VMEM((Z, Y - 1, quarter, 2 * feat), BF16),
            pltpu.VMEM((Z, 2, eighth, 2 * feat), BF16),
            pltpu.VMEM((eighth, 2 * feat), F32),
            pltpu.VMEM((RING - 1, eighth, 2 * feat), BF16),
            dma((6,)),
            dma((64,)),
            dma((8,)),
            dma((8,)),
            dma((8,)),
            dma((Z,)),
            dma((Z,)),
            dma((4,)),
            dma((X - 1,)),
            dma((Z, Y - 1)),
            dma((RING - 1,)),
        ],
        compiler_params=pltpu.CompilerParams(
            collective_id=0, has_side_effects=True, vmem_limit_bytes=48 << 20
        ),
        name="attention_backward",
    )(query, key, value, output, out_grad, lse, block_order)


def solution(mesh):
    in_specs = (
        P("head", "blk", None),
        P("blk", None),
        P("blk", None),
        P("head", "blk", None),
        P("head", "blk", None),
        P("head", "blk"),
        P(),
    )
    out_specs = (P("head", "blk", None), P(("blk", "head"), None), P(("blk", "head"), None))
    return jax.shard_map(
        on_device, mesh=mesh, in_specs=in_specs, out_specs=out_specs, check_vma=False
    )
```

time: 465 us -> 65.5 us (0.14)
  the two profiles are of different devices: /device:TPU:39 before, /device:TPU:1 now
where the time goes in v1:
time: 65.5 us; the launch traced here: 65.3 us
  Pallas kernels  56.9 us (87%)
  local copies, waits for them, and re-layouts  7.78 us (12%)
  between operations  0.66 us (1%)
    pallas_call x1, Pallas kernels, on_device(): pl.pallas_call(kernel, out_shape=(jax.ShapeDtypeStruct((1, rows, feat), F...  56.9 us
    unnamed x17, local copies, waits for them, and re-layouts  7.78 us

profile of v1, /device:TPU:1, one launch (start us, length us, event | category | flops | bytes accessed | tf_op | source)
XLA Modules:
  0.0 65.3 jit_solution(9869476038419221692)
XLA Ops:
  0.6 0.0 copy-start
  0.6 0.9 %copy-done = bf16[1,512,128]{2,1,0:T(8,128)(2,1)S(1)} copy-done((bf16[1,512,128]{2,1,0:T(8,128)(2,1)S(1)}, bf16[1,512,128]{2,1,0:T(8,128)(2,1)}, u32[]{:S(2)}) %copy-start) | copy-done | bytes 131096
  1.5 0.0 copy-start.1
  1.5 0.9 %copy-done.1 = bf16[512,128]{1,0:T(8,128)(2,1)S(1)} copy-done((bf16[512,128]{1,0:T(8,128)(2,1)S(1)}, bf16[512,128]{1,0:T(8,128)(2,1)}, u32[]{:S(2)}) %copy-start.1) | copy-done | bytes 131096
  2.4 0.0 copy-start.2
  2.4 0.9 %copy-done.2 = bf16[512,128]{1,0:T(8,128)(2,1)S(1)} copy-done((bf16[512,128]{1,0:T(8,128)(2,1)S(1)}, bf16[512,128]{1,0:T(8,128)(2,1)}, u32[]{:S(2)}) %copy-start.2) | copy-done | bytes 131096
  3.3 0.0 copy-start.3
  3.3 0.9 %copy-done.3 = bf16[1,512,128]{2,1,0:T(8,128)(2,1)S(1)} copy-done((bf16[1,512,128]{2,1,0:T(8,128)(2,1)S(1)}, bf16[1,512,128]{2,1,0:T(8,128)(2,1)}, u32[]{:S(2)}) %copy-start.3) | copy-done | bytes 131096
  4.3 0.0 copy-start.4
  4.3 0.9 %copy-done.4 = bf16[1,512,128]{2,1,0:T(8,128)(2,1)S(1)} copy-done((bf16[1,512,128]{2,1,0:T(8,128)(2,1)S(1)}, bf16[1,512,128]{2,1,0:T(8,128)(2,1)}, u32[]{:S(2)}) %copy-start.4) | copy-done | bytes 131096
  5.2 0.0 copy-start.5
  5.2 0.7 %copy-done.5 = f32[1,512]{1,0:T(1,128)S(1)} copy-done((f32[1,512]{1,0:T(1,128)S(1)}, f32[1,512]{1,0:T(1,128)}, u32[]{:S(2)}) %copy-start.5) | copy-done | bytes 2072
  5.8 0.0 copy-start.6
  5.8 0.7 %copy-done.6 = s32[64]{0:T(128)S(1)} copy-done((s32[64]{0:T(128)S(1)}, s32[64]{0:T(128)}, u32[]{:S(2)}) %copy-start.6) | copy-done | bytes 280
  6.5 56.9 %attention_backward.1 = (f32[1,512,128]{2,1,0:T(8,128)S(1)}, f32[64,128]{1,0:T(8,128)S(1)}, f32[64,128]{1,0:T(8,128)S(1)}) custom-call(bf16[1,512,128]{2,1,0:T(8,128)(2,1)S(1)} %copy-done, bf16[512,128]{1,0:T(8,128)(2,1)S(1)} %copy-done.1, bf16[512,128]{1,0:T(8,128)(2,1)S(1)} %copy-done.2, bf16[1,512,128]{2,1,0:T(8,128)(2,1)S(1)} %copy-done.3, ...), custom_call_target="tpu_custom_call" | custom-call | tf_op jit(solution)/shard_map/attention_backward/pallas_call | solution.py:351
  63.4 0.7 %copy.13 = f32[1,512,128]{2,1,0:T(8,128)} copy(f32[1,512,128]{2,1,0:T(8,128)S(1)} %get-tuple-element.6) | data formatting | bytes 524288
  64.1 0.6 copy.14
  64.7 0.6 copy.15
Async XLA Ops:
  0.6 0.9 %copy-start = (bf16[1,512,128]{2,1,0:T(8,128)(2,1)S(1)}, bf16[1,512,128]{2,1,0:T(8,128)(2,1)}, u32[]{:S(2)}) copy-start(bf16[1,512,128]{2,1,0:T(8,128)(2,1)} %q_hbm.1) | copy-start | bytes 393220
  1.5 0.9 %copy-start.1 = (bf16[512,128]{1,0:T(8,128)(2,1)S(1)}, bf16[512,128]{1,0:T(8,128)(2,1)}, u32[]{:S(2)}) copy-start(bf16[512,128]{1,0:T(8,128)(2,1)} %k_hbm.1) | copy-start | bytes 393220
  2.4 0.9 %copy-start.2 = (bf16[512,128]{1,0:T(8,128)(2,1)S(1)}, bf16[512,128]{1,0:T(8,128)(2,1)}, u32[]{:S(2)}) copy-start(bf16[512,128]{1,0:T(8,128)(2,1)} %v_hbm.1) | copy-start | bytes 393220
  3.3 0.9 %copy-start.3 = (bf16[1,512,128]{2,1,0:T(8,128)(2,1)S(1)}, bf16[1,512,128]{2,1,0:T(8,128)(2,1)}, u32[]{:S(2)}) copy-start(bf16[1,512,128]{2,1,0:T(8,128)(2,1)} %o_hbm.1) | copy-start | bytes 393220
  4.3 0.9 %copy-start.4 = (bf16[1,512,128]{2,1,0:T(8,128)(2,1)S(1)}, bf16[1,512,128]{2,1,0:T(8,128)(2,1)}, u32[]{:S(2)}) copy-start(bf16[1,512,128]{2,1,0:T(8,128)(2,1)} %g_hbm.1) | copy-start | bytes 393220
  5.2 0.7 %copy-start.5 = (f32[1,512]{1,0:T(1,128)S(1)}, f32[1,512]{1,0:T(1,128)}, u32[]{:S(2)}) copy-start(f32[1,512]{1,0:T(1,128)} %l_hbm.1) | copy-start | bytes 6148
  5.8 0.7 %copy-start.6 = (s32[64]{0:T(128)S(1)}, s32[64]{0:T(128)}, u32[]{:S(2)}) copy-start(s32[64]{0:T(128)} %order.1) | copy-start | bytes 772

commit v2 on v0

v2 whole, which is shorter than its diff:
```python
import jax
import jax.numpy as jnp
from jax import lax
from jax.experimental import pallas as pl
from jax.experimental.pallas import tpu as pltpu
from jax.sharding import PartitionSpec as P

F32 = jnp.float32
BF16 = jnp.bfloat16
MESH = pl.DeviceIdType.MESH
LOG2E = 1.4426950408889634
DEAD = 1.0e9
PAIR = (0, 0, 1, 1, 0, 2, 2, 1, 3, 3, 2, 3, 3, 2, 1, 0)
KEYS = (0, 1, 0, 1, 2, 0, 1, 2, 0, 1, 2, 2, 3, 3, 3, 3)
X, Z, C, Y = 4, 4, 2, 4
RING = 8


def dot(left, right, left_dim, right_dim):
    return lax.dot_general(
        left, right, (((left_dim,), (right_dim,)), ((), ())), preferred_element_type=F32
    )


def kernel(
    q_hbm, k_hbm, v_hbm, o_hbm, g_hbm, l_hbm, order,
    dq_out, dkv_out,
    qb, gb, sb, kb, vb, ob, lb,
    dq_acc, dk_acc, dv_acc, core_in, x_out, x_in,
    y_out, y_own, y_in, z_out, z_in, dq_rows,
    load_sem, send_sem, q_sem, g_sem, s_sem, k_sem, v_sem, core_sem, x_sem, y_sem, z_sem,
):
    rows, feat = ob.shape
    half, piece = rows // 2, rows // RING
    scale = feat ** -0.5
    blk = lax.axis_index("blk")
    head = lax.axis_index("head")
    core = blk % C
    zlo = (blk // C) % Z
    x = blk // (C * Z)
    zhi = head % 2
    y = head // 2
    ring = zhi * Z + zlo

    def at(dx=0, dc=0):
        return {"blk": (((x + dx) % X) * Z + zlo) * C + (core + dc) % C, "head": head}

    def at_y(dy):
        return {"blk": blk, "head": ((y + dy) % Y) * 2 + zhi}

    def at_ring(dz):
        there = (ring + dz) % RING
        return {"blk": (x * Z + there % Z) * C + core, "head": y * 2 + there // Z}

    greeted = (
        [at(dc=1)] + [at(dx=i) for i in (1, 2, 3)] + [at_y(i) for i in (1, 2, 3)]
        + [at_ring(i) for i in range(1, RING)]
    )
    barrier = pltpu.get_barrier_semaphore()
    for device in greeted:
        pl.semaphore_signal(barrier, inc=1, device_id=device, device_id_type=MESH)

    loads = []
    own = pl.ds(0, rows)
    for src, dst in (
        (g_hbm.at[0], gb.at[0, own]), (o_hbm.at[0], ob), (l_hbm, lb), (q_hbm.at[0], qb.at[0, own]),
        (k_hbm.at[:, 0], kb.at[0, 0]), (v_hbm.at[:, 0], vb.at[0, 0]),
        (k_hbm.at[:, 1], kb.at[0, 1]), (v_hbm.at[:, 1], vb.at[0, 1]),
    ):
        loads.append(pltpu.make_async_copy(src, dst, load_sem.at[len(loads)]))
        loads[-1].start()

    sends = []

    def remote(src, dst, recv, device):
        copy = pltpu.make_async_remote_copy(
            src_ref=src, dst_ref=dst, send_sem=send_sem.at[len(sends)], recv_sem=recv,
            device_id=device, device_id_type=MESH,
        )
        sends.append(copy)
        return copy

    def landed(dst, recv):
        pltpu.make_async_remote_copy(
            src_ref=dst, dst_ref=dst, send_sem=send_sem.at[0], recv_sem=recv,
            device_id=at(dc=1), device_id_type=MESH,
        ).wait_recv()

    def start(copies):
        for copy in copies:
            copy.start()

    def part(buf, place):
        p, first, count = place
        return buf.at[p, pl.ds(first, count)]

    def stat(place):
        p, first, count = place
        return sb.at[p, :, pl.ds(first, count)]

    def pass_q(src, dst, i, device):
        return remote(part(qb, src), part(qb, dst), q_sem.at[i], device)

    def pass_g(src, dst, i, device):
        return remote(part(gb, src), part(gb, dst), g_sem.at[i], device)

    def pass_s(src, dst, i, device):
        return remote(stat(src), stat(dst), s_sem.at[i], device)

    def pass_all(src, dst, i, device):
        return [f(src, dst, i, device) for f in (pass_q, pass_g, pass_s)]

    def got(place, i):
        landed(part(qb, place), q_sem.at[i])
        landed(part(gb, place), g_sem.at[i])
        landed(stat(place), s_sem.at[i])

    def got_keys(r, h):
        landed(kb.at[r, h], k_sem.at[r, h])
        landed(vb.at[r, h], v_sem.at[r, h])

    to_core = pass_all((0, 0, rows), (0, rows, rows), 0, at(dc=1))
    waves, keys_out, forward, relay_x, relay_z = [], [], [], [], []
    for w in (0, 1):
        mine, p, i = (0, w * half, half), 1 + w, 3 * w + 1
        right = pass_all(mine, (p, half, half), i + 1, at(dx=1))
        left = pass_all(mine, (p, 0, half), i, at(dx=3))
        waves.append((right, left))
        keys_out.append([
            remote(buf.at[0, w], buf.at[p, h], sem.at[p, h], at_ring(dz))
            for buf, sem in ((kb, k_sem), (vb, v_sem)) for h, dz in ((1, 1), (0, 7))
        ])
        forward.append(pass_all((p, 0, rows), (p, rows, rows), i + 2, at(dc=1)))
        far = (3, w * half, half)
        relay_x.append([
            pass_q((p, 0, half), far, 7 + w, at(dx=3)),
            pass_g((p, half, half), far, 7 + w, at(dx=1)),
            pass_s((p, 0, half), far, 7 + w, at(dx=3)),
        ])
        relay_z.append([
            remote(buf.at[p, w], buf.at[3, w], sem.at[3, w], at_ring((7, 1)[w]))
            for buf, sem in ((kb, k_sem), (vb, v_sem))
        ])
    forward_far = pass_all((3, 0, rows), (3, rows, rows), 9, at(dc=1))
    dq_core = [remote(dq_acc.at[p, 1], core_in.at[p], core_sem.at[p], at(dc=1)) for p in range(4)]
    dq_x = [None] + [
        [remote(x_out.at[w, i], x_in.at[2 * i, w], x_sem.at[2 * i, w], at(dx=(1, 3)[i])) for i in (0, 1)]
        for w in (0, 1)
    ] + [[remote(x_out.at[2, w], x_in.at[1, w], x_sem.at[1, w], at(dx=2)) for w in (0, 1)]]
    kv_y = [
        [remote(y_out.at[r, (y + i) % Y], y_in.at[r, i - 1], y_sem.at[r, i - 1], at_y(i)) for i in (2, 1, 3)]
        for r in range(4)
    ]
    kv_z = [[remote(z_out.at[0, 1 - zhi], z_in.at[Z - 1], z_sem.at[Z - 1], at_ring(Z))]]
    for r, targets in ((1, ((1, 0), (3, 0))), (2, ((1, 1), (3, 1))), (3, ((2, 0), (2, 1)))):
        kv_z.append([])
        for h, (dz, side) in enumerate(targets):
            ahead = (side * Z + (zlo + dz) % Z - ring + RING) % RING
            kv_z[r].append(
                remote(z_out.at[r, h], z_in.at[ahead - 1], z_sem.at[ahead - 1], at_ring(ahead))
            )

    for i in (0, 1, 2):
        loads[i].wait()
    delta = jnp.sum(jnp.transpose(gb[0, own].astype(F32) * ob[...].astype(F32)), axis=0, keepdims=True)
    sb[0, 0:1, own] = lb[...] * LOG2E
    sb[0, 1:2, own] = delta
    for i in range(3, 8):
        loads[i].wait()
    pl.semaphore_wait(barrier, len(greeted))

    start(to_core[:2])
    for w in (0, 1):
        right, left = waves[w]
        start([right[0], left[0], right[1], left[1]])
        start(keys_out[w])
        if w == 0:
            dq_acc[...] = jnp.zeros_like(dq_acc)
            start([to_core[2]])
        start([right[2], left[2]])
    dk_acc[...] = jnp.zeros_like(dk_acc)
    dv_acc[...] = jnp.zeros_like(dv_acc)

    def block(dx, dc, dz, b):
        return order[2 * (((x + dx) % X * Z + (zlo + dz) % Z) * C + (core + dc) % C) + b]

    def grads(r, keys, vals, q_rows, g_rows, probs, d_row):
        dprobs = dot(vals, g_rows, 1, 1)
        dscores = (probs * (dprobs - d_row)).astype(BF16)
        dv_acc[r] += dot(probs.astype(BF16), g_rows, 1, 0).reshape(2, Y, piece, feat)
        dk_acc[r] += dot(dscores, q_rows, 1, 0).reshape(2, Y, piece, feat)
        return dot(keys, dscores, 0, 0)

    def biased(l_row, q_blocks, k_block):
        parts = []
        for i, q_block in enumerate(q_blocks):
            dead = jnp.where(q_block > k_block, 0.0, DEAD)
            parts.append(l_row[:, i * half : (i + 1) * half] + dead)
        return jnp.concatenate(parts, axis=1)

    def tile(r, p, first, count, q_blocks, k_blocks):
        cols = pl.ds(first * rows, count * rows)
        keys, vals = kb[r].reshape(rows, feat), vb[r].reshape(rows, feat)
        q_rows, g_rows = qb[p, cols], gb[p, cols]
        l_row, d_row = sb[p, 0:1, cols], sb[p, 1:2, cols]
        lows = jnp.stack([biased(l_row, q_blocks, b) for b in k_blocks])
        scores = dot(keys, q_rows, 1, 1).reshape(4, half // 2, count * rows)
        probs = jnp.exp2(scores * (scale * LOG2E) - lows).reshape(rows, count * rows)
        part_q = grads(r, keys, vals, q_rows, g_rows, probs, d_row)
        for i in range(count):
            dq_acc[p, first + i] += part_q[:, i * rows : (i + 1) * rows]

    own_blocks = [block(0, 0, 0, b) for b in (0, 1)]
    q_rows, g_rows = qb[0, own], gb[0, own]
    at_row = lax.broadcasted_iota(jnp.int32, (rows, 1), 0)
    at_col = lax.broadcasted_iota(jnp.int32, (1, rows), 1)
    quarter = at_row % half // piece
    k_off = quarter % 2 * (2 * piece) + at_row // half * piece + at_row % piece
    k_pos = jnp.where(quarter < 2, own_blocks[0], own_blocks[1]) * half + k_off
    q_pos = jnp.where(at_col < half, own_blocks[0], own_blocks[1]) * half + at_col % half
    keys, vals = kb[0].reshape(rows, feat), vb[0].reshape(rows, feat)
    scores = dot(keys, q_rows, 1, 1)
    probs = jnp.where(
        q_pos >= k_pos, jnp.exp2(scores * (scale * LOG2E) - sb[0, 0:1, own]), 0.0
    )
    dq_acc[0, 0] += grads(0, keys, vals, q_rows, g_rows, probs, sb[0, 1:2, own])

    got((0, rows, rows), 0)
    tile(0, 0, 1, 1, [block(0, 1, 0, b) for b in (0, 1)], own_blocks * 2)

    def stage_row(r):
        for h in (0, 1):
            y_out[r, :, h, :, :feat] = dk_acc[r, h].astype(BF16)
            y_out[r, :, h, :, feat:] = dv_acc[r, h].astype(BF16)
            y_own[r, h, :, :feat] = dk_acc[r, h, y]
            y_own[r, h, :, feat:] = dv_acc[r, h, y]

    def sum_y(r):
        total = y_own[r]
        for i in range(Y - 1):
            landed(y_in.at[r, i], y_sem.at[r, i])
            total = total + y_in[r, i].astype(F32)
        z_out[r] = total.astype(BF16)
        if r == 0:
            y_own[0] = total

    def join_core(p):
        landed(core_in.at[p], core_sem.at[p])
        total = (dq_acc[p, 0] + core_in[p]).astype(BF16)
        x_out[p - 1, 0] = total[:, :half]
        x_out[p - 1, 1] = total[:, half:]

    before = {
        1: lambda: (
            got((1, 0, half), 1), got((1, half, half), 2), start(forward[0]), start(relay_x[0]),
            got_keys(1, 0), start(relay_z[0]), got_keys(1, 1),
        ),
        2: lambda: got((1, rows, rows), 3),
        3: lambda: (
            got((2, 0, half), 4), got((2, half, half), 5), start(forward[1]), start(relay_x[1]),
        ),
        4: lambda: (got_keys(2, 1), start(relay_z[1]), got_keys(2, 0)),
        5: lambda: got((2, rows, rows), 6),
        6: lambda: (got((3, 0, half), 7), got((3, half, half), 8), start(forward_far)),
        8: lambda: got((3, rows, rows), 9),
        12: lambda: (got_keys(3, 0), got_keys(3, 1)),
    }
    after = {
        8: lambda: stage_row(0),
        9: lambda: (start(kv_y[0]), stage_row(1)),
        10: lambda: start(kv_y[1]),
        11: lambda: stage_row(2),
        12: lambda: (start(kv_y[2]), sum_y(0), dq_core[3].start()),
        13: lambda: (sum_y(1), start(kv_z[0]), dq_core[2].start(), join_core(3)),
        14: lambda: (start(dq_x[3]), start(kv_z[1]), dq_core[1].start(), join_core(2)),
        15: lambda: (start(dq_x[2]), dq_core[0].start(), stage_row(3)),
    }

    def chosen(t, table):
        out = jnp.int32(table[1])
        for i in range(2, len(table)):
            out = jnp.where(t == i, table[i], out)
        return out

    def step(t, carry):
        p, r = chosen(t, PAIR), chosen(t, KEYS)
        for i, action in before.items():
            @pl.when(t == i)
            def _():
                action()

        near, far = (p + 1) // 2, (r + 1) // 2
        mid = near % 2
        q_blocks = [
            block((near, 4 - near)[j % 2], j // 2, 0, j % 2 * (1 - mid) + mid * (p - 1)) for j in range(4)
        ]
        k_blocks = [block(0, 0, (far, 4 - far)[h], b) for h in (0, 1) for b in (0, 1)]
        tile(r, p, 0, 2, q_blocks, k_blocks)

        for i, action in after.items():
            @pl.when(t == i)
            def _():
                action()

        return carry

    lax.fori_loop(1, 16, step, 0)

    sum_y(2)
    start(kv_y[3])
    start(kv_z[2])
    join_core(1)
    landed(core_in.at[0], core_sem.at[0])
    total = dq_acc[0, 0] + core_in[0]
    start(dq_x[1])
    for w in (0, 1):
        side = total[:, w * half : (w + 1) * half]
        for i in (1, 0, 2):
            landed(x_in.at[i, w], x_sem.at[i, w])
            side = side + x_in[i, w].astype(F32)
        dq_rows[w] = jnp.transpose(side * scale)
    dq_leave = pltpu.make_async_copy(dq_rows, dq_out.at[0], load_sem.at[0])
    sum_y(3)
    dq_leave.start()
    total = y_own[0, zhi]
    for i in (4, 1, 5, 3, 7):
        landed(z_in.at[i - 1], z_sem.at[i - 1])
        total = total + z_in[i - 1].astype(F32)
    start(kv_z[3])
    for i in (2, 6):
        landed(z_in.at[i - 1], z_sem.at[i - 1])
        total = total + z_in[i - 1].astype(F32)
    dkv_out[0] = total[:, :feat] * scale
    dkv_out[1] = total[:, feat:]
    dq_leave.wait()
    for copy in sends:
        copy.wait_send()


def finish(dq_in, dkv_in, dq_out, dk_out, dv_out, held, held_kv, in_sem, out_sem):
    half = held.shape[1]
    moves = [
        (dq_in.at[0, w], held.at[w], dq_out.at[0, pl.ds(w * half, half)]) for w in (0, 1)
    ] + [(dkv_in.at[i], held_kv.at[i], out) for i, out in enumerate((dk_out, dv_out))]
    arrivals = [
        pltpu.make_async_copy(src, at, in_sem.at[i]) for i, (src, at, _) in enumerate(moves)
    ]
    leaves = [
        pltpu.make_async_copy(at, dst, out_sem.at[i]) for i, (_, at, dst) in enumerate(moves)
    ]
    for copy in arrivals:
        copy.start()
    for arrival, leave in zip(arrivals, leaves):
        arrival.wait()
        leave.start()
    for leave in leaves:
        leave.wait()


def on_device(query, key, value, output, out_grad, lse, block_order):
    rows, feat = key.shape
    half, piece = rows // 2, rows // RING
    any_space = pl.BlockSpec(memory_space=pl.ANY)
    vmem = pl.BlockSpec(memory_space=pltpu.VMEM)
    dma = pltpu.SemaphoreType.DMA
    dq, dkv = pl.pallas_call(
        kernel,
        out_shape=(
            jax.ShapeDtypeStruct((1, 2, half, feat), F32),
            jax.ShapeDtypeStruct((2, piece, feat), F32),
        ),
        in_specs=[any_space] * 6 + [pl.BlockSpec(memory_space=pltpu.SMEM)],
        out_specs=(any_space, vmem),
        scratch_shapes=[
            pltpu.VMEM((4, 2 * rows, feat), BF16),
            pltpu.VMEM((4, 2 * rows, feat), BF16),
            pltpu.VMEM((4, 2, 2 * rows), F32),
            pltpu.VMEM((4, 2, Y, piece, feat), BF16),
            pltpu.VMEM((4, 2, Y, piece, feat), BF16),
            pltpu.VMEM((rows, feat), BF16),
            pltpu.VMEM((1, rows), F32),
            pltpu.VMEM((4, 2, feat, rows), F32),
            pltpu.VMEM((4, 2, Y, piece, feat), F32),
            pltpu.VMEM((4, 2, Y, piece, feat), F32),
            pltpu.VMEM((4, feat, rows), F32),
            pltpu.VMEM((3, 2, feat, half), BF16),
            pltpu.VMEM((3, 2, feat, half), BF16),
            pltpu.VMEM((4, Y, 2, piece, 2 * feat), BF16),
            pltpu.VMEM((4, 2, piece, 2 * feat), F32),
            pltpu.VMEM((4, Y - 1, 2, piece, 2 * feat), BF16),
            pltpu.VMEM((4, 2, piece, 2 * feat), BF16),
            pltpu.VMEM((RING - 1, piece, 2 * feat), BF16),
            pltpu.VMEM((2, half, feat), F32),
            dma((8,)),
            dma((80,)),
            dma((10,)),
            dma((10,)),
            dma((10,)),
            dma((4, 2)),
            dma((4, 2)),
            dma((4,)),
            dma((3, 2)),
            dma((4, Y - 1)),
            dma((RING - 1,)),
        ],
        compiler_params=pltpu.CompilerParams(
            collective_id=0, has_side_effects=True, vmem_limit_bytes=67043328
        ),
        name="attention_backward",
    )(
        query,
        key.reshape(Y, 2, piece, feat),
        value.reshape(Y, 2, piece, feat),
        output, out_grad, lse, block_order,
    )
    return pl.pallas_call(
        finish,
        out_shape=(
            jax.ShapeDtypeStruct((1, rows, feat), F32),
            jax.ShapeDtypeStruct((piece, feat), F32),
            jax.ShapeDtypeStruct((piece, feat), F32),
        ),
        in_specs=[any_space] * 2,
        out_specs=(any_space,) * 3,
        scratch_shapes=[
            pltpu.VMEM((2, half, feat), F32),
            pltpu.VMEM((2, piece, feat), F32),
            dma((4,)),
            dma((4,)),
        ],
        compiler_params=pltpu.CompilerParams(vmem_limit_bytes=67043328),
        name="finish",
    )(dq, dkv)


def solution(mesh):
    in_specs = (
        P("head", "blk", None),
        P("blk", None),
        P("blk", None),
        P("head", "blk", None),
        P("head", "blk", None),
        P("head", "blk"),
        P(),
    )
    out_specs = (P("head", "blk", None), P(("blk", "head"), None), P(("blk", "head"), None))
    return jax.shard_map(
        on_device, mesh=mesh, in_specs=in_specs, out_specs=out_specs, check_vma=False
    )
```

time: 465 us -> 58.6 us (0.13)
  the two profiles are of different devices: /device:TPU:39 before, /device:TPU:1 now
where the time goes in v2:
time: 58.6 us; the launch traced here: 58.4 us
  Pallas kernels  57.8 us (99%)
  between operations  0.64 us (1%)
    pallas_call x1, Pallas kernels, on_device(): pl.pallas_call(kernel, out_shape=(jax.ShapeDtypeStruct((1, 2, half, feat)...  56.1 us
    pallas_call x1, Pallas kernels, on_device(): pl.pallas_call(finish, out_shape=(jax.ShapeDtypeStruct((1, rows, feat), F...  1.71 us

profile of v2, /device:TPU:1, one launch (start us, length us, event | category | flops | bytes accessed | tf_op | source)
XLA Modules:
  0.0 58.4 jit_solution(11625899479135704543)
XLA Ops:
  0.6 56.1 %attention_backward.1 = (f32[1,2,256,128]{3,2,1,0:T(8,128)}, f32[2,64,128]{2,1,0:T(8,128)}) custom-call(bf16[1,512,128]{2,1,0:T(8,128)(2,1)} %q_hbm.1, bf16[4,2,64,128]{3,2,1,0:T(8,128)(2,1)} %bitcast.2, bf16[4,2,64,128]{3,2,1,0:T(8,128)(2,1)} %bitcast.3, bf16[1,512,128]{2,1,0:T(8,128)(2,1)} %o_hbm.1, bf16[1,512,128]{2,1,0:T(8,128)(2,1)} %g_hbm.1, ...), custom_call_target="tpu_custom_call" | custom-call | tf_op jit(solution)/shard_map/attention_backward/pallas_call | solution.py:366
  56.7 1.7 %finish.1 = (f32[1,512,128]{2,1,0:T(8,128)}, f32[64,128]{1,0:T(8,128)}, f32[64,128]{1,0:T(8,128)}) custom-call(f32[1,2,256,128]{3,2,1,0:T(8,128)} %get-tuple-element.5.dq_in, f32[2,64,128]{2,1,0:T(8,128)} %get-tuple-element.6.dkv_in), custom_call_target="tpu_custom_call" | custom-call | tf_op jit(solution)/shard_map/finish/pallas_call | solution.py:416

commit v3 on v2

--- a/solution.py
+++ b/solution.py
@@ -28,7 +28,7 @@
     qb, gb, sb, kb, vb, ob, lb,
     dq_acc, dk_acc, dv_acc, core_in, x_out, x_in,
     y_out, y_own, y_in, z_out, z_in, dq_rows,
-    load_sem, send_sem, q_sem, g_sem, s_sem, k_sem, v_sem, core_sem, x_sem, y_sem, z_sem,
+    load_sem, send_sem, q_sem, g_sem, s_sem, k_sem, v_sem, core_sem, x_sem, y_sem, z_sem, round_sem,
 ):
     rows, feat = ob.shape
     half, piece = rows // 2, rows // RING
@@ -52,10 +52,8 @@
         there = (ring + dz) % RING
         return {"blk": (x * Z + there % Z) * C + core, "head": y * 2 + there // Z}
 
-    greeted = (
-        [at(dc=1)] + [at(dx=i) for i in (1, 2, 3)] + [at_y(i) for i in (1, 2, 3)]
-        + [at_ring(i) for i in range(1, RING)]
-    )
+    beside = [at(dx=1), at(dx=3), at_y(1), at_y(3), at_ring(1), at_ring(7)]
+    greeted = [at(dc=1)] + beside
     barrier = pltpu.get_barrier_semaphore()
     for device in greeted:
         pl.semaphore_signal(barrier, inc=1, device_id=device, device_id_type=MESH)
@@ -85,6 +83,13 @@
             src_ref=dst, dst_ref=dst, send_sem=send_sem.at[0], recv_sem=recv,
             device_id=at(dc=1), device_id_type=MESH,
         ).wait_recv()
+
+    def send_round(i):
+        for device in (beside, beside[4:], beside[4:])[i]:
+            pl.semaphore_signal(round_sem.at[i], inc=1, device_id=device, device_id_type=MESH)
+
+    def wait_round(i):
+        pl.semaphore_wait(round_sem.at[i], (6, 2, 2)[i])
 
     def start(copies):
         for copy in copies:
@@ -178,6 +183,7 @@
             dq_acc[...] = jnp.zeros_like(dq_acc)
             start([to_core[2]])
         start([right[2], left[2]])
+    send_round(0)
     dk_acc[...] = jnp.zeros_like(dk_acc)
     dv_acc[...] = jnp.zeros_like(dv_acc)
 
@@ -259,9 +265,9 @@
         3: lambda: (
             got((2, 0, half), 4), got((2, half, half), 5), start(forward[1]), start(relay_x[1]),
         ),
-        4: lambda: (got_keys(2, 1), start(relay_z[1]), got_keys(2, 0)),
-        5: lambda: got((2, rows, rows), 6),
-        6: lambda: (got((3, 0, half), 7), got((3, half, half), 8), start(forward_far)),
+        4: lambda: (wait_round(0), send_round(1), got_keys(2, 1), start(relay_z[1]), got_keys(2, 0)),
+        5: lambda: (wait_round(1), send_round(2), got((2, rows, rows), 6)),
+        6: lambda: (wait_round(2), got((3, 0, half), 7), got((3, half, half), 8), start(forward_far)),
         8: lambda: got((3, rows, rows), 9),
         12: lambda: (got_keys(3, 0), got_keys(3, 1)),
     }
@@ -270,10 +276,10 @@
         9: lambda: (start(kv_y[0]), stage_row(1)),
         10: lambda: start(kv_y[1]),
         11: lambda: stage_row(2),
-        12: lambda: (start(kv_y[2]), sum_y(0), dq_core[3].start()),
-        13: lambda: (sum_y(1), start(kv_z[0]), dq_core[2].start(), join_core(3)),
-        14: lambda: (start(dq_x[3]), start(kv_z[1]), dq_core[1].start(), join_core(2)),
-        15: lambda: (start(dq_x[2]), dq_core[0].start(), stage_row(3)),
+        12: lambda: (start(kv_y[2]), dq_core[3].start()),
+        13: lambda: dq_core[2].start(),
+        14: lambda: (dq_core[1].start(), join_core(3), sum_y(0), start(dq_x[3])),
+        15: lambda: (dq_core[0].start(), join_core(2), stage_row(3)),
     }
 
     def chosen(t, table):
@@ -306,13 +312,17 @@
 
     lax.fori_loop(1, 16, step, 0)
 
+    sum_y(1)
+    start(kv_y[3])
+    start(dq_x[2])
+    start(kv_z[0])
+    start(kv_z[1])
+    join_core(1)
     sum_y(2)
-    start(kv_y[3])
+    start(dq_x[1])
     start(kv_z[2])
-    join_core(1)
     landed(core_in.at[0], core_sem.at[0])
     total = dq_acc[0, 0] + core_in[0]
-    start(dq_x[1])
     for w in (0, 1):
         side = total[:, w * half : (w + 1) * half]
         for i in (1, 0, 2):
@@ -402,6 +412,7 @@
             dma((3, 2)),
             dma((4, Y - 1)),
             dma((RING - 1,)),
+            pltpu.SemaphoreType.REGULAR((3,)),
         ],
         compiler_params=pltpu.CompilerParams(
             collective_id=0, has_side_effects=True, vmem_limit_bytes=67043328

time: 58.6 us -> 56.4 us (0.962)
  Pallas kernels: 57.8 us -> 55.6 us
    pallas_call x1, Pallas kernels: 56.1 us -> 53.9 us  [on_device(): pl.pallas_call(kernel, out_shape=(jax.ShapeDtypeStruct((1, 2, half, feat)...]
where the time goes in v3:
time: 56.4 us; the launch traced here: 56.3 us
  Pallas kernels  55.6 us (99%)
  between operations  0.64 us (1%)
    pallas_call x1, Pallas kernels, on_device(): pl.pallas_call(kernel, out_shape=(jax.ShapeDtypeStruct((1, 2, half, feat)...  53.9 us
    pallas_call x1, Pallas kernels, on_device(): pl.pallas_call(finish, out_shape=(jax.ShapeDtypeStruct((1, rows, feat), F...  1.71 us

profile of v3, /device:TPU:1, one launch (start us, length us, event | category | flops | bytes accessed | tf_op | source)
XLA Modules:
  0.0 56.3 jit_solution(4346541476192883542)
XLA Ops:
  0.6 53.9 %attention_backward.1 = (f32[1,2,256,128]{3,2,1,0:T(8,128)}, f32[2,64,128]{2,1,0:T(8,128)}) custom-call(bf16[1,512,128]{2,1,0:T(8,128)(2,1)} %q_hbm.1, bf16[4,2,64,128]{3,2,1,0:T(8,128)(2,1)} %bitcast.2, bf16[4,2,64,128]{3,2,1,0:T(8,128)(2,1)} %bitcast.3, bf16[1,512,128]{2,1,0:T(8,128)(2,1)} %o_hbm.1, bf16[1,512,128]{2,1,0:T(8,128)(2,1)} %g_hbm.1, ...), custom_call_target="tpu_custom_call" | custom-call | tf_op jit(solution)/shard_map/attention_backward/pallas_call | solution.py:376
  54.5 1.7 %finish.1 = (f32[1,512,128]{2,1,0:T(8,128)}, f32[64,128]{1,0:T(8,128)}, f32[64,128]{1,0:T(8,128)}) custom-call(f32[1,2,256,128]{3,2,1,0:T(8,128)} %get-tuple-element.5.dq_in, f32[2,64,128]{2,1,0:T(8,128)} %get-tuple-element.6.dkv_in), custom_call_target="tpu_custom_call" | custom-call | tf_op jit(solution)/shard_map/finish/pallas_call | solution.py:427

commit v4 on v3

--- a/solution.py
+++ b/solution.py
@@ -10,8 +10,8 @@
 MESH = pl.DeviceIdType.MESH
 LOG2E = 1.4426950408889634
 DEAD = 1.0e9
-PAIR = (0, 0, 1, 1, 0, 2, 2, 1, 3, 3, 2, 3, 3, 2, 1, 0)
-KEYS = (0, 1, 0, 1, 2, 0, 1, 2, 0, 1, 2, 2, 3, 3, 3, 3)
+PAIR = (0, 0, 1, 1, 0, 2, 2, 1, 3, 3, 2, 3, 3, 2)
+KEYS = (0, 1, 0, 1, 2, 0, 1, 2, 0, 1, 2, 2, 3, 3)
 X, Z, C, Y = 4, 4, 2, 4
 RING = 8
 
@@ -154,7 +154,16 @@
     ] + [[remote(x_out.at[2, w], x_in.at[1, w], x_sem.at[1, w], at(dx=2)) for w in (0, 1)]]
     kv_y = [
         [remote(y_out.at[r, (y + i) % Y], y_in.at[r, i - 1], y_sem.at[r, i - 1], at_y(i)) for i in (2, 1, 3)]
-        for r in range(4)
+        for r in range(3)
+    ]
+    kv_y_last = [
+        [
+            remote(
+                y_out.at[3, (y + i) % Y, h], y_in.at[3, i - 1, h], y_sem.at[3 + h, i - 1], at_y(i)
+            )
+            for i in (2, 1, 3)
+        ]
+        for h in (0, 1)
     ]
     kv_z = [[remote(z_out.at[0, 1 - zhi], z_in.at[Z - 1], z_sem.at[Z - 1], at_ring(Z))]]
     for r, targets in ((1, ((1, 0), (3, 0))), (2, ((1, 1), (3, 1))), (3, ((2, 0), (2, 1)))):
@@ -190,11 +199,12 @@
     def block(dx, dc, dz, b):
         return order[2 * (((x + dx) % X * Z + (zlo + dz) % Z) * C + (core + dc) % C) + b]
 
-    def grads(r, keys, vals, q_rows, g_rows, probs, d_row):
+    def grads(kv_at, keys, vals, q_rows, g_rows, probs, d_row):
         dprobs = dot(vals, g_rows, 1, 1)
         dscores = (probs * (dprobs - d_row)).astype(BF16)
-        dv_acc[r] += dot(probs.astype(BF16), g_rows, 1, 0).reshape(2, Y, piece, feat)
-        dk_acc[r] += dot(dscores, q_rows, 1, 0).reshape(2, Y, piece, feat)
+        shape = dv_acc.at[kv_at].shape
+        dv_acc[kv_at] += dot(probs.astype(BF16), g_rows, 1, 0).reshape(shape)
+        dk_acc[kv_at] += dot(dscores, q_rows, 1, 0).reshape(shape)
         return dot(keys, dscores, 0, 0)
 
     def biased(l_row, q_blocks, k_block):
@@ -204,15 +214,15 @@
             parts.append(l_row[:, i * half : (i + 1) * half] + dead)
         return jnp.concatenate(parts, axis=1)
 
-    def tile(r, p, first, count, q_blocks, k_blocks):
+    def tile(kv_at, p, first, count, q_blocks, k_blocks):
         cols = pl.ds(first * rows, count * rows)
-        keys, vals = kb[r].reshape(rows, feat), vb[r].reshape(rows, feat)
+        keys, vals = kb[kv_at].reshape(-1, feat), vb[kv_at].reshape(-1, feat)
         q_rows, g_rows = qb[p, cols], gb[p, cols]
         l_row, d_row = sb[p, 0:1, cols], sb[p, 1:2, cols]
         lows = jnp.stack([biased(l_row, q_blocks, b) for b in k_blocks])
-        scores = dot(keys, q_rows, 1, 1).reshape(4, half // 2, count * rows)
-        probs = jnp.exp2(scores * (scale * LOG2E) - lows).reshape(rows, count * rows)
-        part_q = grads(r, keys, vals, q_rows, g_rows, probs, d_row)
+        scores = dot(keys, q_rows, 1, 1).reshape(len(k_blocks), half // 2, count * rows)
+        probs = jnp.exp2(scores * (scale * LOG2E) - lows).reshape(-1, count * rows)
+        part_q = grads(kv_at, keys, vals, q_rows, g_rows, probs, d_row)
         for i in range(count):
             dq_acc[p, first + i] += part_q[:, i * rows : (i + 1) * rows]
 
@@ -229,17 +239,20 @@
     probs = jnp.where(
         q_pos >= k_pos, jnp.exp2(scores * (scale * LOG2E) - sb[0, 0:1, own]), 0.0
     )
-    dq_acc[0, 0] += grads(0, keys, vals, q_rows, g_rows, probs, sb[0, 1:2, own])
+    dq_acc[0, 0] += grads((0,), keys, vals, q_rows, g_rows, probs, sb[0, 1:2, own])
 
     got((0, rows, rows), 0)
-    tile(0, 0, 1, 1, [block(0, 1, 0, b) for b in (0, 1)], own_blocks * 2)
+    tile((0,), 0, 1, 1, [block(0, 1, 0, b) for b in (0, 1)], own_blocks * 2)
+
+    def stage(r, h):
+        y_out[r, :, h, :, :feat] = dk_acc[r, h].astype(BF16)
+        y_out[r, :, h, :, feat:] = dv_acc[r, h].astype(BF16)
+        y_own[r, h, :, :feat] = dk_acc[r, h, y]
+        y_own[r, h, :, feat:] = dv_acc[r, h, y]
 
     def stage_row(r):
-        for h in (0, 1):
-            y_out[r, :, h, :, :feat] = dk_acc[r, h].astype(BF16)
-            y_out[r, :, h, :, feat:] = dv_acc[r, h].astype(BF16)
-            y_own[r, h, :, :feat] = dk_acc[r, h, y]
-            y_own[r, h, :, feat:] = dv_acc[r, h, y]
+        stage(r, 0)
+        stage(r, 1)
 
     def sum_y(r):
         total = y_own[r]
@@ -249,6 +262,13 @@
         z_out[r] = total.astype(BF16)
         if r == 0:
             y_own[0] = total
+
+    def sum_y_last(h):
+        total = y_own[3, h]
+        for i in range(Y - 1):
+            landed(y_in.at[3, i, h], y_sem.at[3 + h, i])
+            total = total + y_in[3, i, h].astype(F32)
+        z_out[3, h] = total.astype(BF16)
 
     def join_core(p):
         landed(core_in.at[p], core_sem.at[p])
@@ -277,9 +297,13 @@
         10: lambda: start(kv_y[1]),
         11: lambda: stage_row(2),
         12: lambda: (start(kv_y[2]), dq_core[3].start()),
-        13: lambda: dq_core[2].start(),
-        14: lambda: (dq_core[1].start(), join_core(3), sum_y(0), start(dq_x[3])),
-        15: lambda: (dq_core[0].start(), join_core(2), stage_row(3)),
+        13: lambda: (dq_core[2].start(), sum_y(0)),
+    }
+    after_half = {
+        0: lambda: (start(kv_z[0]), join_core(3)),
+        1: lambda: (start(dq_x[3]), stage(3, 0)),
+        2: lambda: (dq_core[1].start(), start(kv_y_last[0]), join_core(2)),
+        3: lambda: (start(dq_x[2]), dq_core[0].start(), stage(3, 1)),
     }
 
     def chosen(t, table):
@@ -287,6 +311,13 @@
         for i in range(2, len(table)):
             out = jnp.where(t == i, table[i], out)
         return out
+
+    def pair_blocks(p):
+        near = (p + 1) // 2
+        mid = near % 2
+        return [
+            block((near, 4 - near)[j % 2], j // 2, 0, j % 2 * (1 - mid) + mid * (p - 1)) for j in range(4)
+        ]
 
     def step(t, carry):
         p, r = chosen(t, PAIR), chosen(t, KEYS)
@@ -295,13 +326,9 @@
             def _():
                 action()
 
-        near, far = (p + 1) // 2, (r + 1) // 2
-        mid = near % 2
-        q_blocks = [
-            block((near, 4 - near)[j % 2], j // 2, 0, j % 2 * (1 - mid) + mid * (p - 1)) for j in range(4)
-        ]
+        far = (r + 1) // 2
         k_blocks = [block(0, 0, (far, 4 - far)[h], b) for h in (0, 1) for b in (0, 1)]
-        tile(r, p, 0, 2, q_blocks, k_blocks)
+        tile((r,), p, 0, 2, pair_blocks(p), k_blocks)
 
         for i, action in after.items():
             @pl.when(t == i)
@@ -310,33 +337,46 @@
 
         return carry
 
-    lax.fori_loop(1, 16, step, 0)
+    lax.fori_loop(1, len(PAIR), step, 0)
+
+    def half_step(t, carry):
+        p, h = 1 - t % 2, t // 2
+        tile((3, h), p, 0, 2, pair_blocks(p), [block(0, 0, 2, b) for b in (0, 1)])
+        for i, action in after_half.items():
+            @pl.when(t == i)
+            def _():
+                action()
+
+        return carry
+
+    lax.fori_loop(0, 4, half_step, 0)
 
     sum_y(1)
-    start(kv_y[3])
-    start(dq_x[2])
-    start(kv_z[0])
+    start(kv_y_last[1])
     start(kv_z[1])
     join_core(1)
     sum_y(2)
     start(dq_x[1])
     start(kv_z[2])
+    sum_y_last(0)
     landed(core_in.at[0], core_sem.at[0])
-    total = dq_acc[0, 0] + core_in[0]
+    dq_acc[0, 0, :, :half] += core_in[0, :, :half]
+    start(kv_z[3][:1])
+    sum_y_last(1)
+    dq_acc[0, 0, :, half:] += core_in[0, :, half:]
+    start(kv_z[3][1:])
     for w in (0, 1):
-        side = total[:, w * half : (w + 1) * half]
+        side = dq_acc[0, 0, :, w * half : (w + 1) * half]
         for i in (1, 0, 2):
             landed(x_in.at[i, w], x_sem.at[i, w])
             side = side + x_in[i, w].astype(F32)
         dq_rows[w] = jnp.transpose(side * scale)
-    dq_leave = pltpu.make_async_copy(dq_rows, dq_out.at[0], load_sem.at[0])
-    sum_y(3)
-    dq_leave.start()
     total = y_own[0, zhi]
     for i in (4, 1, 5, 3, 7):
         landed(z_in.at[i - 1], z_sem.at[i - 1])
         total = total + z_in[i - 1].astype(F32)
-    start(kv_z[3])
+    dq_leave = pltpu.make_async_copy(dq_rows, dq_out.at[0], load_sem.at[0])
+    dq_leave.start()
     for i in (2, 6):
         landed(z_in.at[i - 1], z_sem.at[i - 1])
         total = total + z_in[i - 1].astype(F32)
@@ -410,7 +450,7 @@
             dma((4, 2)),
             dma((4,)),
             dma((3, 2)),
-            dma((4, Y - 1)),
+            dma((5, Y - 1)),
             dma((RING - 1,)),
             pltpu.SemaphoreType.REGULAR((3,)),
         ],

time: 56.4 us -> 52.2 us (0.926)
  Pallas kernels: 55.6 us -> 51.4 us
    pallas_call x1, Pallas kernels: 53.9 us -> 49.7 us  [on_device(): pl.pallas_call(kernel, out_shape=(jax.ShapeDtypeStruct((1, 2, half, feat)...]
where the time goes in v4:
time: 52.2 us; the launch traced here: 52.1 us
  Pallas kernels  51.4 us (98%)
  between operations  0.64 us (1%)
    pallas_call x1, Pallas kernels, on_device(): pl.pallas_call(kernel, out_shape=(jax.ShapeDtypeStruct((1, 2, half, feat)...  49.7 us
    pallas_call x1, Pallas kernels, on_device(): pl.pallas_call(finish, out_shape=(jax.ShapeDtypeStruct((1, rows, feat), F...  1.71 us

profile of v4, /device:TPU:1, one launch (start us, length us, event | category | flops | bytes accessed | tf_op | source)
XLA Modules:
  0.0 52.1 jit_solution(10857687533188477995)
XLA Ops:
  0.6 49.7 %attention_backward.1 = (f32[1,2,256,128]{3,2,1,0:T(8,128)}, f32[2,64,128]{2,1,0:T(8,128)}) custom-call(bf16[1,512,128]{2,1,0:T(8,128)(2,1)} %q_hbm.1, bf16[4,2,64,128]{3,2,1,0:T(8,128)(2,1)} %bitcast.2, bf16[4,2,64,128]{3,2,1,0:T(8,128)(2,1)} %bitcast.3, bf16[1,512,128]{2,1,0:T(8,128)(2,1)} %o_hbm.1, bf16[1,512,128]{2,1,0:T(8,128)(2,1)} %g_hbm.1, ...), custom_call_target="tpu_custom_call" | custom-call | tf_op jit(solution)/shard_map/attention_backward/pallas_call | solution.py:416
  50.4 1.7 %finish.1 = (f32[1,512,128]{2,1,0:T(8,128)}, f32[64,128]{1,0:T(8,128)}, f32[64,128]{1,0:T(8,128)}) custom-call(f32[1,2,256,128]{3,2,1,0:T(8,128)} %get-tuple-element.5.dq_in, f32[2,64,128]{2,1,0:T(8,128)} %get-tuple-element.6.dkv_in), custom_call_target="tpu_custom_call" | custom-call | tf_op jit(solution)/shard_map/finish/pallas_call | solution.py:467

commit v5 on v4

--- a/solution.py
+++ b/solution.py
@@ -183,15 +183,16 @@
         loads[i].wait()
     pl.semaphore_wait(barrier, len(greeted))
 
-    start(to_core[:2])
-    for w in (0, 1):
+    def send_wave(w):
         right, left = waves[w]
         start([right[0], left[0], right[1], left[1]])
         start(keys_out[w])
-        if w == 0:
-            dq_acc[...] = jnp.zeros_like(dq_acc)
-            start([to_core[2]])
         start([right[2], left[2]])
+
+    start(to_core[:2])
+    send_wave(0)
+    start([to_core[2]])
+    dq_acc[...] = jnp.zeros_like(dq_acc)
     send_round(0)
     dk_acc[...] = jnp.zeros_like(dk_acc)
     dv_acc[...] = jnp.zeros_like(dv_acc)
@@ -243,6 +244,7 @@
 
     got((0, rows, rows), 0)
     tile((0,), 0, 1, 1, [block(0, 1, 0, b) for b in (0, 1)], own_blocks * 2)
+    send_wave(1)
 
     def stage(r, h):
         y_out[r, :, h, :, :feat] = dk_acc[r, h].astype(BF16)

time: 52.2 us -> 51.1 us (0.979)
  Pallas kernels: 51.4 us -> 50.3 us
    pallas_call x1, Pallas kernels: 49.7 us -> 48.6 us  [on_device(): pl.pallas_call(kernel, out_shape=(jax.ShapeDtypeStruct((1, 2, half, feat)...]
where the time goes in v5:
time: 51.1 us; the launch traced here: 51 us
  Pallas kernels  50.3 us (98%)
  between operations  0.64 us (1%)
    pallas_call x1, Pallas kernels, on_device(): pl.pallas_call(kernel, out_shape=(jax.ShapeDtypeStruct((1, 2, half, feat)...  48.6 us
    pallas_call x1, Pallas kernels, on_device(): pl.pallas_call(finish, out_shape=(jax.ShapeDtypeStruct((1, rows, feat), F...  1.71 us

profile of v5, /device:TPU:1, one launch (start us, length us, event | category | flops | bytes accessed | tf_op | source)
XLA Modules:
  0.0 51.0 jit_solution(4871547206799840660)
XLA Ops:
  0.6 48.6 %attention_backward.1 = (f32[1,2,256,128]{3,2,1,0:T(8,128)}, f32[2,64,128]{2,1,0:T(8,128)}) custom-call(bf16[1,512,128]{2,1,0:T(8,128)(2,1)} %q_hbm.1, bf16[4,2,64,128]{3,2,1,0:T(8,128)(2,1)} %bitcast.2, bf16[4,2,64,128]{3,2,1,0:T(8,128)(2,1)} %bitcast.3, bf16[1,512,128]{2,1,0:T(8,128)(2,1)} %o_hbm.1, bf16[1,512,128]{2,1,0:T(8,128)(2,1)} %g_hbm.1, ...), custom_call_target="tpu_custom_call" | custom-call | tf_op jit(solution)/shard_map/attention_backward/pallas_call | solution.py:418
  49.3 1.7 %finish.1 = (f32[1,512,128]{2,1,0:T(8,128)}, f32[64,128]{1,0:T(8,128)}, f32[64,128]{1,0:T(8,128)}) custom-call(f32[1,2,256,128]{3,2,1,0:T(8,128)} %get-tuple-element.5.dq_in, f32[2,64,128]{2,1,0:T(8,128)} %get-tuple-element.6.dkv_in), custom_call_target="tpu_custom_call" | custom-call | tf_op jit(solution)/shard_map/finish/pallas_call | solution.py:469

commit v6 on v5

--- a/solution.py
+++ b/solution.py
@@ -379,13 +379,16 @@
         total = total + z_in[i - 1].astype(F32)
     dq_leave = pltpu.make_async_copy(dq_rows, dq_out.at[0], load_sem.at[0])
     dq_leave.start()
+    for copy in sends:
+        if all(copy is not last for last in kv_z[3]):
+            copy.wait_send()
     for i in (2, 6):
         landed(z_in.at[i - 1], z_sem.at[i - 1])
         total = total + z_in[i - 1].astype(F32)
     dkv_out[0] = total[:, :feat] * scale
     dkv_out[1] = total[:, feat:]
     dq_leave.wait()
-    for copy in sends:
+    for copy in kv_z[3]:
         copy.wait_send()
 
 

time: 51.1 us -> 51 us (level)
  no operation moved by 1% of the time
where the time goes in v6:
time: 51 us; the launch traced here: 50.9 us
  Pallas kernels  50.2 us (98%)
  between operations  0.64 us (1%)
    pallas_call x1, Pallas kernels, on_device(): pl.pallas_call(kernel, out_shape=(jax.ShapeDtypeStruct((1, 2, half, feat)...  48.5 us
    pallas_call x1, Pallas kernels, on_device(): pl.pallas_call(finish, out_shape=(jax.ShapeDtypeStruct((1, rows, feat), F...  1.71 us

profile of v6, /device:TPU:1, one launch (start us, length us, event | category | flops | bytes accessed | tf_op | source)
XLA Modules:
  0.0 50.9 jit_solution(8202618632479320359)
XLA Ops:
  0.6 48.5 %attention_backward.1 = (f32[1,2,256,128]{3,2,1,0:T(8,128)}, f32[2,64,128]{2,1,0:T(8,128)}) custom-call(bf16[1,512,128]{2,1,0:T(8,128)(2,1)} %q_hbm.1, bf16[4,2,64,128]{3,2,1,0:T(8,128)(2,1)} %bitcast.2, bf16[4,2,64,128]{3,2,1,0:T(8,128)(2,1)} %bitcast.3, bf16[1,512,128]{2,1,0:T(8,128)(2,1)} %o_hbm.1, bf16[1,512,128]{2,1,0:T(8,128)(2,1)} %g_hbm.1, ...), custom_call_target="tpu_custom_call" | custom-call | tf_op jit(solution)/shard_map/attention_backward/pallas_call | solution.py:421
  49.2 1.7 %finish.1 = (f32[1,512,128]{2,1,0:T(8,128)}, f32[64,128]{1,0:T(8,128)}, f32[64,128]{1,0:T(8,128)}) custom-call(f32[1,2,256,128]{3,2,1,0:T(8,128)} %get-tuple-element.5.dq_in, f32[2,64,128]{2,1,0:T(8,128)} %get-tuple-element.6.dkv_in), custom_call_target="tpu_custom_call" | custom-call | tf_op jit(solution)/shard_map/finish/pallas_call | solution.py:472
